TPU v7x, 128 devices: a whole 4x4x4 slice. The times are simulated.
128 devices in a mesh: gx: 4 (over z_lo, core), gy: 4 (over x), gz: 8 (over z_hi, y).
Axes of the slice: x: 4, y: 4, z: 4 (z_hi: 2, z_lo: 2; z = z_hi * 2 + z_lo), core: 2. Of those that a mesh axis runs over, the one named last changes fastest.
Arguments:
- right_sides: float32 [2, 128, 1024, 1024], P(None, ('gx', 'gy', 'gz')), may hold values from -6 to 6
- projector: float32 [2, 128, 1024, 192], P(None, ('gx', 'gy', 'gz')), may hold values from -0.1875 to 0.1875
- mixing: float32 [8, 2, 128, 2, 192, 192], P(None, None, ('gx', 'gy', 'gz')), may hold values from -0.3125 to 0.3125
- expander: float32 [256, 1024, 192], P(('gx', 'gy', 'gz')), may hold values from -0.4375 to 0.4375
Outputs:
- product: float32 [256, 1024, 1024], P(('gx', 'gy', 'gz'))
All inputs are finite; a program needn't handle non-finite values.
Results may differ from a plain program's by a relative error of at most 0.0001.
Values sent between devices are 32-bit elements; how exact they have to be, the bound alone decides.
No kernel may reach another device: no remote copies, remote signals or barrier semaphores. Data moves between devices by JAX's collectives and lax.ppermute only.
A program may use at most 128 MiB of HBM per device.

v0:
```python
import functools

import jax
import jax.numpy as jnp
from jax import lax
from jax.experimental import pallas as pl
from jax.experimental.pallas import tpu as pltpu
from jax.sharding import PartitionSpec as P

AXES = ("gx", "gy", "gz")
DEVICES = 128
Y0, Y1, ZH, X0, X1, CORE, Z0, SLOT = range(8)
WIDTHS = (512, 512)
VMEM_LIMIT = 56 * 2**20
HIGH = lax.Precision.HIGH
FAST_LEVELS = (0, 1, 2, 4, 5, 6, 7)
EXACT = lax.Precision.HIGHEST


def parity(own, mask):
    total = jnp.int32(0)
    for bit in range(7):
        if (mask >> bit) & 1:
            total = total ^ (jnp.right_shift(own, bit) & 1)
    return total


def ordered(pair, swap):
    chosen = swap == 1
    return jnp.where(chosen, pair[1], pair[0]), jnp.where(chosen, pair[0], pair[1])


class Place:
    def __init__(self, held=tuple(range(8)), mask=0):
        self.held, self.mask = tuple(held), mask

    def traded(self, *swaps):
        held = list(self.held)
        for one, other in swaps:
            held[one], held[other] = held[other], held[one]
        return held

    def to(self, held):
        coming = self.held.index(held[SLOT])
        leaving = held.index(self.held[SLOT])
        routes = []
        for t in range(2):
            pairs = []
            for device in range(DEVICES):
                value = ((device >> coming) & 1) ^ t if coming != SLOT else 0
                reached = 0
                for position in range(7):
                    bit = held[position]
                    if position == leaving:
                        reached |= value << position
                    else:
                        reached |= ((device >> self.held.index(bit)) & 1) << position
                pairs.append((device, reached))
            routes.append(pairs)
        if coming == SLOT:
            mask = 0
            for position in range(7):
                if (self.mask >> self.held.index(held[position])) & 1:
                    mask |= 1 << position
            return Place(held, mask), 0, routes
        return Place(held, 1 << leaving), self.mask ^ (1 << coming), routes


def sent(values, pairs):
    if all(source == reached for source, reached in pairs):
        return values
    return lax.ppermute(values, AXES, pairs)


def after(values, awaited):
    return lax.optimization_barrier((values, awaited))[0]


def halves(x):
    high = x.astype(jnp.bfloat16)
    low = (x - high.astype(jnp.float32)).astype(jnp.bfloat16)
    return high, low


def product(left, right, transposed=False):
    (lh, ll), (rh, rl) = left, right
    axis = 1 if transposed else 0
    dims = (((0 if transposed else 1,), (0,)), ((), ()))
    rows = lh.shape[axis]
    dot = functools.partial(lax.dot_general, dimension_numbers=dims, preferred_element_type=jnp.float32)
    both = dot(jnp.concatenate([lh, ll], axis=axis), rh)
    return both[:rows] + both[rows:] + dot(lh, rl)


def params(flops, moved_bytes):
    return dict(
        compiler_params=pltpu.CompilerParams(vmem_limit_bytes=VMEM_LIMIT),
        cost_estimate=pl.CostEstimate(flops=flops, transcendentals=0, bytes_accessed=moved_bytes),
    )


def pick(flag, first, second):
    return jnp.where(flag == 1, second, first)


def expand_kernel(flag, e_ref, r0_ref, r1_ref, *rest):
    out_ref = rest[-1]
    chosen = pl.program_id(0) ^ flag[0]
    right = halves(pick(chosen, r0_ref[...], r1_ref[...]))
    out_ref[0] = product(halves(e_ref[0]), right, transposed=True)


def expand(flag, expander, pair, start, total, earlier):
    rank, width = pair[0].shape
    leaf = expander.shape[2]
    rows = min(leaf, 512)
    base = start // width
    r_spec = pl.BlockSpec((rank, width), lambda e, i, f: (0, 0))
    extra = () if earlier is None else (earlier,)
    return pl.pallas_call(
        expand_kernel,
        grid_spec=pltpu.PrefetchScalarGridSpec(
            num_scalar_prefetch=1,
            grid=(2, leaf // rows),
            in_specs=[pl.BlockSpec((1, rank, rows), lambda e, i, f: (e, 0, i)), r_spec, r_spec]
            + [pl.BlockSpec(memory_space=pl.ANY)] * len(extra),
            out_specs=pl.BlockSpec((1, rows, width), lambda e, i, f: (e, i, base)),
        ),
        out_shape=jax.ShapeDtypeStruct((2, leaf, total), jnp.float32),
        input_output_aliases={} if earlier is None else {4: 0},
        name="expand",
        **params(4 * leaf * rank * width, 8 * leaf * (rank + width) + 8 * rank * width),
    )(flag, expander, *pair, *extra)


HOME = Place()
FLIP_CORE = [(d, d ^ (1 << CORE)) for d in range(DEVICES)]
MOVES = (
    (((SLOT, Y0), (CORE, Y1)), ((0, False),)),
    (((SLOT, CORE),), ((1, False),)),
    (((SLOT, Y1), (CORE, Y0)), ()),
    (((SLOT, ZH), (CORE, Z0)), ((2, False),)),
    (((SLOT, X1), (CORE, X0)), ((3, True), (4, False))),
    (((SLOT, ZH), (CORE, X0)), ((5, False),)),
    (((SLOT, CORE),), ((6, False),)),
    (((SLOT, Y0), (CORE, Y1)), ()),
    (((SLOT, Z0),), ((7, False),)),
)


def places():
    found, at_level, place = [], {}, HOME
    for trades, levels in MOVES:
        held = place.traded(*trades)
        place = place.to(held)[0]
        found.append(place)
        for level, _ in levels:
            at_level[level] = place
    return found, at_level


def fetch(mixing, own, levels, held):
    place, order, routes = HOME.to(held)
    chosen = mixing[levels, :, 0]
    bit = parity(own, order)
    pair = [lax.dynamic_index_in_dim(chosen, bit ^ t, 1, keepdims=False) for t in range(2)]
    return [sent(v, r) for v, r in zip(pair, routes)], place


def local_factors(pair, swap, shift):
    first, second = ordered(pair, swap ^ shift)
    own_first, cross_first = ordered((first[0], first[1]), swap)
    cross_second, own_second = ordered((second[1], second[0]), swap)
    return (
        jnp.concatenate([own_first, cross_second], axis=0),
        jnp.concatenate([cross_first, own_second], axis=0),
    )


def dot(a, b, level):
    return jnp.dot(a, b, precision=HIGH if level in FAST_LEVELS else EXACT)


def shards(right_sides, projector, mixing, expander):
    own = lax.axis_index(AXES)
    total = right_sides.shape[3]
    rank = projector.shape[3]
    _, at_level = places()
    factors = {}

    def get(levels, held_at):
        pair, place = fetch(mixing, own, slice(levels[0], levels[-1] + 1), held_at)
        for index, level in enumerate(levels):
            factors[level] = ([v[index] for v in pair], place)
        return pair, place

    get((0,), list(at_level[0].held))
    get((1,), list(at_level[1].held))
    pair, place = get((2, 3, 4), list(at_level[2].held))
    place, order, routes = place.to(list(at_level[3].held))
    pair = ordered([v[1:] for v in pair], parity(own, order))
    pair = [sent(v, r) for v, r in zip(pair, routes)]
    for index, level in enumerate((3, 4)):
        factors[level] = ([v[index] for v in pair], place)
    get((5,), list(at_level[5].held))
    get((6,), list(at_level[6].held))
    late_mixing = mixing

    chunks, starts, start = [], [], 0
    place = HOME
    for width in WIDTHS:
        columns = slice(start, start + width)
        chunks.append(
            [
                lax.dot_general(
                    projector[c, 0],
                    right_sides[c, 0, :, columns],
                    (((0,), (0,)), ((), ())),
                    precision=HIGH,
                )
                for c in range(2)
            ]
        )
        starts.append(start)
        start += width
    sorted_for = 0
    for number, (trades, levels) in enumerate(MOVES):
        place_next, order, routes = place.to(place.traded(*trades))
        if order != sorted_for:
            chunks = [ordered(pair, parity(own, order ^ sorted_for)) for pair in chunks]
        chunks = [[sent(v, r) for v, r in zip(pair, routes)] for pair in chunks]
        place = place_next
        sorted_for = 0
        if number + 1 < len(MOVES):
            following = place.to(place.traded(*MOVES[number + 1][0]))[1]
        else:
            following = place.mask
        for position, (level, at_core) in enumerate(levels):
            if level == 2:
                late_mixing = after(mixing, chunks[-1][1])
                pair7, place7 = fetch(late_mixing, own, slice(7, 8), list(at_level[7].held))
                factors[7] = ([v[0] for v in pair7], place7)
            pair_w, place_w = factors[level]
            assert place_w.held == place.held, (level, place_w.held, place.held)
            shift = parity(own, place.mask ^ place_w.mask)
            last = position + 1 == len(levels)
            swap_mask = following if last else 0
            swap = parity(own, swap_mask)
            if at_core:
                aligned = ordered(pair_w, shift)
                for index, pair in enumerate(chunks):
                    others = [sent(v, FLIP_CORE) for v in pair]
                    out = [dot(w[0], v, level) + dot(w[1], o, level) for w, v, o in zip(aligned, pair, others)]
                    chunks[index] = ordered(out, swap) if swap_mask else out
            else:
                for_first, for_second = local_factors(pair_w, swap, shift)
                for index, pair in enumerate(chunks):
                    out = dot(for_first, pair[0], level) + dot(for_second, pair[1], level)
                    chunks[index] = [out[:rank], out[rank:]]
            if last:
                sorted_for = swap_mask
    assert sorted_for == place.mask
    flag = jnp.zeros((1,), jnp.int32)
    result = None
    for start, pair in zip(starts, chunks):
        result = expand(flag, jnp.swapaxes(expander, 1, 2), pair, start, total, result)
    return result


def solution(mesh):
    placed = (
        P(None, AXES, None, None),
        P(None, AXES, None, None),
        P(None, None, AXES, None, None, None),
        P(AXES, None, None),
    )
    return jax.shard_map(
        shards, mesh=mesh, in_specs=placed, out_specs=P(AXES, None, None), check_vma=False
    )
```

profile of v0, /device:TPU:7, one launch (start us, length us, event | category | flops | bytes accessed | tf_op | source)
XLA Modules:
  0.0 239.9 jit_solution(18071109728839059966)
XLA Ops:
  0.0 2.8 %fusion.4 = f32[192,512]{1,0:T(8,128)S(1)} fusion(f32[2,1,1024,1024]{3,2,1,0:T(8,128)} %param.4, f32[2,1,1024,192]{2,3,1,0:T(8,128)} %param.5), kind=kOutput, calls=%fused_computation.4 | convolution fusion | flops 603979776 | bytes 3276800 | tf_op jit(solution)/shard_map/dot_general | solution.py:215
  2.8 3.4 %broadcast_select_fusion.9 = (f32[192,512]{1,0:T(8,128)}, f32[192,512]{1,0:T(8,128)}) fusion(f32[192,512]{1,0:T(8,128)S(1)} %fusion.4, pred[]{:T(512)S(6)} %eq.59, f32[2,1,1024,1024]{3,2,1,0:T(8,128)} %param.4, f32[2,1,1024,192]{2,3,1,0:T(8,128)S(1)} %copy-done), kind=kOutput, calls=%fused_computation.133 | convolution fusion | flops 604176384 | bytes 4063233 | tf_op jit(solution)/shard_map/dot_general | solution.py:215
  6.2 5.4 %collective-permute-start.4 = (f32[192,512]{1,0:T(8,128)}, f32[192,512]{1,0:T(8,128)S(1)}, u32[]{:S(2)}, u32[]{:S(2)}) collective-permute-start(f32[192,512]{1,0:T(8,128)} %get-tuple-element.59), channel_id=1, source_target_pairs={{0,0},{1,1},{2,32},{3,33},{4,4},{5,5},{6,36},{7,37},{8,8},{9,9},{1... | collective-permute-start | bytes 1179656 | tf_op jit(solution)/shard_map/ppermute | solution.py:72
  11.6 3.3 %fusion.74 = (f32[1,2,1,2,192,192]{5,4,3,2,1,0:T(8,128)}, f32[1,2,1,2,192,192]{5,4,3,2,1,0:T(8,128)S(1)}, f32[1,2,1,2,192,192]{5,4,3,2,1,0:T(8,128)}, f32[1,2,1,2,192,192]{5,4,3,2,1,0:T(8,128)S(1)}) fusion(f32[8,2,1,2,192,192]{5,4,3,2,1,0:T(8,128)} %param.6), kind=kLoop, calls=%fused_computation.174 | loop fusion | bytes 4718592 | tf_op jit(solution)/shard_map/slice | solution.py:164
  14.9 2.1 dynamic-slice_bitcast_fusion.5
  17.0 4.6 %collective-permute-start.12 = (f32[1,2,192,192]{3,2,1,0:T(8,128)}, f32[1,2,192,192]{3,2,1,0:T(8,128)}, u32[]{:S(2)}, u32[]{:S(2)}) collective-permute-start(f32[1,2,192,192]{3,2,1,0:T(8,128)} %get-tuple-element.41), channel_id=1, source_target_pairs={{0,64},{1,65},{2,66},{3,67},{4,80},{5,81},{6,82},{7,83},{8,72},{9,... | collective-permute-start | bytes 884744 | tf_op jit(solution)/shard_map/ppermute | solution.py:72
  21.6 3.1 %collective-permute-start.13 = (f32[1,2,192,192]{3,2,1,0:T(8,128)}, f32[1,2,192,192]{3,2,1,0:T(8,128)}, u32[]{:S(2)}, u32[]{:S(2)}) collective-permute-start(f32[1,2,192,192]{3,2,1,0:T(8,128)} %get-tuple-element.42), channel_id=1, source_target_pairs={{0,0},{1,1},{2,2},{3,3},{4,16},{5,17},{6,18},{7,19},{8,8},{9,9},{1... | collective-permute-start | bytes 884744 | tf_op jit(solution)/shard_map/ppermute | solution.py:72
  24.7 0.9 dynamic-slice_bitcast_fusion.7
  25.7 1.1 collective-permute-start.2
  26.7 3.3 %collective-permute-start.3 = (f32[1,2,192,192]{3,2,1,0:T(8,128)}, f32[1,2,192,192]{3,2,1,0:T(8,128)}, u32[]{:S(2)}, u32[]{:S(2)}) collective-permute-start(f32[1,2,192,192]{3,2,1,0:T(8,128)} %get-tuple-element.64), channel_id=1, source_target_pairs={{0,0},{1,1},{2,32},{3,33},{4,4},{5,5},{6,36},{7,37},{8,8},{9,9},{1... | collective-permute-start | bytes 884744 | tf_op jit(solution)/shard_map/ppermute | solution.py:72
  30.1 2.5 %fusion = f32[192,512]{1,0:T(8,128)S(1)} fusion(f32[2,1,1024,1024]{3,2,1,0:T(8,128)} %param.4, f32[2,1,1024,192]{2,3,1,0:T(8,128)S(1)} %copy-done), kind=kOutput, calls=%fused_computation | convolution fusion | flops 603979776 | bytes 3276800 | tf_op jit(solution)/shard_map/dot_general | solution.py:215
  32.6 1.4 copy-done.1
  34.0 3.5 %broadcast_select_fusion.7 = (f32[192,512]{1,0:T(8,128)}, f32[192,512]{1,0:T(8,128)}) fusion(f32[192,512]{1,0:T(8,128)S(1)} %fusion, pred[]{:T(512)S(6)} %eq.59, f32[2,1,1024,1024]{3,2,1,0:T(8,128)} %param.4, f32[2,1,1024,192]{2,3,1,0:T(8,128)S(1)} %copy-done.1), kind=kOutput, calls=%fused_computation.131 | convolution fusion | flops 604176384 | bytes 4063233 | tf_op jit(solution)/shard_map/dot_general | solution.py:215
  37.5 2.0 dynamic-slice_bitcast_fusion.9
  39.6 1.7 dynamic-slice_bitcast_fusion
  42.1 3.6 %collective-permute-start.1 = (f32[1,2,192,192]{3,2,1,0:T(8,128)}, f32[1,2,192,192]{3,2,1,0:T(8,128)S(1)}, u32[]{:S(2)}, u32[]{:S(2)}) collective-permute-start(f32[1,2,192,192]{3,2,1,0:T(8,128)} %get-tuple-element.58), channel_id=1, source_target_pairs={{0,0},{1,32},{2,1},{3,33},{4,4},{5,36},{6,5},{7,37},{8,8},{9,40},{... | collective-permute-start | bytes 884744 | tf_op jit(solution)/shard_map/ppermute | solution.py:72
  45.7 1.2 broadcast_select_fusion.3
  46.9 1.2 collective-permute-start.14
  48.0 5.9 %collective-permute-start.15 = (f32[1,2,192,192]{3,2,1,0:T(8,128)S(1)}, f32[1,2,192,192]{3,2,1,0:T(8,128)S(1)}, u32[]{:S(2)}, u32[]{:S(2)}) collective-permute-start(f32[1,2,192,192]{3,2,1,0:T(8,128)S(1)} %get-tuple-element.48), channel_id=1, source_target_pairs={{0,0},{1,1},{2,2},{3,3},{4,16},{5,17},{6,18},{7,19},{8,8},{9,9},{1... | collective-permute-start | bytes 884744 | tf_op jit(solution)/shard_map/ppermute | solution.py:72
  53.9 1.2 broadcast_select_fusion.11
  55.2 1.2 collective-permute-start.5
  56.5 2.1 collective-permute-start.31
  58.7 4.2 %collective-permute-done.14 = f32[1,2,192,192]{3,2,1,0:T(8,128)S(1)} collective-permute-done((f32[1,2,192,192]{3,2,1,0:T(8,128)S(1)}, f32[1,2,192,192]{3,2,1,0:T(8,128)S(1)}, u32[]{:S(2)}, u32[]{:S(2)}) %collective-permute-start.14) | collective-permute-done | bytes 294944 | tf_op jit(solution)/shard_map/ppermute | solution.py:72
  62.9 1.5 collective-permute-start.32
  64.4 5.4 %collective-permute-done.15 = f32[1,2,192,192]{3,2,1,0:T(8,128)S(1)} collective-permute-done((f32[1,2,192,192]{3,2,1,0:T(8,128)S(1)}, f32[1,2,192,192]{3,2,1,0:T(8,128)S(1)}, u32[]{:S(2)}, u32[]{:S(2)}) %collective-permute-start.15) | collective-permute-done | bytes 294944 | tf_op jit(solution)/shard_map/ppermute | solution.py:72
  70.0 1.0 copy-done.2
  71.1 2.1 collective-permute-start.16
  76.9 0.8 collective-permute-done.6
  78.2 3.6 %collective-permute-start.8 = (f32[192,512]{1,0:T(8,128)S(1)}, f32[192,512]{1,0:T(8,128)S(1)}, u32[]{:S(2)}, u32[]{:S(2)}) collective-permute-start(f32[192,512]{1,0:T(8,128)S(1)} %get-tuple-element.53), channel_id=1, source_target_pairs={{0,2},{1,34},{2,0},{3,32},{4,6},{5,38},{6,4},{7,36},{8,10},{9,42},... | collective-permute-start | bytes 1179656 | tf_op jit(solution)/shard_map/ppermute | solution.py:72
  81.9 2.1 collective-permute-start.7
  84.5 0.9 collective-permute-start.34
  85.5 12.2 %collective-permute-done.17 = f32[3,2,192,192]{3,2,1,0:T(8,128)S(1)} collective-permute-done((f32[3,2,192,192]{3,2,1,0:T(8,128)S(1)}, f32[3,2,192,192]{3,2,1,0:T(8,128)S(1)}, u32[]{:S(2)}, u32[]{:S(2)}) %collective-permute-start.17) | collective-permute-done | bytes 884768 | tf_op jit(solution)/shard_map/ppermute | solution.py:72
  97.6 2.1 collective-permute-start.35
  100.5 0.8 collective-permute-start.19
  101.5 4.7 %collective-permute-start.20 = (f32[192,512]{1,0:T(8,128)S(1)}, f32[192,512]{1,0:T(8,128)S(1)}, u32[]{:S(2)}, u32[]{:S(2)}) collective-permute-start(f32[192,512]{1,0:T(8,128)S(1)} %get-tuple-element.51), channel_id=1, source_target_pairs={{0,0},{1,1},{2,2},{3,3},{4,4},{5,5},{6,6},{7,7},{8,8},{9,9},{10,10... | collective-permute-start | bytes 1179656 | tf_op jit(solution)/shard_map/ppermute | solution.py:72
  106.3 2.0 collective-permute-start.9
  108.4 3.0 %collective-permute-start.36 = (f32[192,512]{1,0:T(8,128)S(1)}, f32[192,512]{1,0:T(8,128)S(1)}, u32[]{:S(2)}, u32[]{:S(2)}) collective-permute-start(f32[192,512]{1,0:T(8,128)S(1)} %get-tuple-element.29), channel_id=1, source_target_pairs={{0,0},{1,1},{2,2},{3,3},{4,4},{5,5},{6,6},{7,7},{8,8},{9,9},{10,10... | collective-permute-start | bytes 1179656 | tf_op jit(solution)/shard_map/ppermute | solution.py:72
  111.4 7.5 %collective-permute-done.18 = f32[2,2,192,192]{3,2,1,0:T(8,128)S(1)} collective-permute-done((f32[2,2,192,192]{3,2,1,0:T(8,128)S(1)}, f32[2,2,192,192]{3,2,1,0:T(8,128)S(1)}, u32[]{:S(2)}, u32[]{:S(2)}) %collective-permute-start.18) | collective-permute-done | bytes 589856 | tf_op jit(solution)/shard_map/ppermute | solution.py:72
  118.9 3.3 %collective-permute-start.37 = (f32[192,512]{1,0:T(8,128)S(1)}, f32[192,512]{1,0:T(8,128)S(1)}, u32[]{:S(2)}, u32[]{:S(2)}) collective-permute-start(f32[192,512]{1,0:T(8,128)S(1)} %get-tuple-element.30), channel_id=1, source_target_pairs={{0,4},{1,5},{2,6},{3,7},{4,0},{5,1},{6,2},{7,3},{8,12},{9,13},{10,... | collective-permute-start | bytes 1179656 | tf_op jit(solution)/shard_map/ppermute | solution.py:72
  122.3 6.5 %collective-permute-start.10 = (f32[1,2,192,192]{3,2,1,0:T(8,128)S(1)}, f32[1,2,192,192]{3,2,1,0:T(8,128)S(1)}, u32[]{:S(2)}, u32[]{:S(2)}) collective-permute-start(f32[1,2,192,192]{3,2,1,0:T(8,128)S(1)} %get-tuple-element.7), channel_id=1, source_target_pairs={{0,0},{1,64},{2,32},{3,96},{4,16},{5,80},{6,48},{7,112},{8,8},{9,7... | collective-permute-start | bytes 884744 | tf_op jit(solution)/shard_map/ppermute | solution.py:72
  129.9 2.3 collective-permute-done.37
  134.0 3.0 %collective-permute-start.23 = (f32[192,512]{1,0:T(8,128)S(1)}, f32[192,512]{1,0:T(8,128)S(1)}, u32[]{:S(2)}, u32[]{:S(2)}) collective-permute-start(f32[192,512]{1,0:T(8,128)S(1)} %get-tuple-element.49), channel_id=1, source_target_pairs={{0,16},{1,17},{2,18},{3,19},{4,20},{5,21},{6,22},{7,23},{8,48},{9,... | collective-permute-start | bytes 1179656 | tf_op jit(solution)/shard_map/ppermute | solution.py:72
  137.1 0.7 collective-permute-start.21
  137.8 4.7 %collective-permute-done.10 = f32[1,2,192,192]{3,2,1,0:T(8,128)S(1)} collective-permute-done((f32[1,2,192,192]{3,2,1,0:T(8,128)S(1)}, f32[1,2,192,192]{3,2,1,0:T(8,128)S(1)}, u32[]{:S(2)}, u32[]{:S(2)}) %collective-permute-start.10) | collective-permute-done | bytes 294944 | tf_op jit(solution)/shard_map/ppermute | solution.py:72
  142.4 12.4 %collective-permute-start.11 = (f32[1,2,192,192]{3,2,1,0:T(8,128)S(1)}, f32[1,2,192,192]{3,2,1,0:T(8,128)S(1)}, u32[]{:S(2)}, u32[]{:S(2)}) collective-permute-start(f32[1,2,192,192]{3,2,1,0:T(8,128)S(1)} %get-tuple-element.8), channel_id=1, source_target_pairs={{0,0},{1,64},{2,32},{3,96},{4,16},{5,80},{6,48},{7,112},{8,8},{9,7... | collective-permute-start | bytes 884744 | tf_op jit(solution)/shard_map/ppermute | solution.py:72
  155.5 0.8 collective-permute-done.23
  162.1 1.6 collective-permute-start.26
  165.8 0.9 collective-permute-start.42
  166.7 1.5 collective-permute-start.43
  168.2 6.4 %collective-permute-done.26 = f32[192,512]{1,0:T(8,128)S(1)} collective-permute-done((f32[192,512]{1,0:T(8,128)S(1)}, f32[192,512]{1,0:T(8,128)S(1)}, u32[]{:S(2)}, u32[]{:S(2)}) %collective-permute-start.26) | collective-permute-done | bytes 393248 | tf_op jit(solution)/shard_map/ppermute | solution.py:72
  175.6 7.4 %collective-permute-done.43 = f32[192,512]{1,0:T(8,128)S(1)} collective-permute-done((f32[192,512]{1,0:T(8,128)S(1)}, f32[192,512]{1,0:T(8,128)S(1)}, u32[]{:S(2)}, u32[]{:S(2)}) %collective-permute-start.43) | collective-permute-done | bytes 393248 | tf_op jit(solution)/shard_map/ppermute | solution.py:72
  184.1 5.3 %collective-permute-start.44 = (f32[192,512]{1,0:T(8,128)S(1)}, f32[192,512]{1,0:T(8,128)S(1)}, u32[]{:S(2)}, u32[]{:S(2)}) collective-permute-start(f32[192,512]{1,0:T(8,128)S(1)} %slice.418), channel_id=1, source_target_pairs={{0,32},{1,33},{2,34},{3,35},{4,36},{5,37},{6,38},{7,39},{8,40},{9,... | collective-permute-start | bytes 1179656 | tf_op jit(solution)/shard_map/ppermute | solution.py:72
  190.5 0.9 collective-permute-done.27
  191.8 6.7 %collective-permute-start.28 = (f32[192,512]{1,0:T(8,128)S(1)}, f32[192,512]{1,0:T(8,128)S(1)}, u32[]{:S(2)}, u32[]{:S(2)}) collective-permute-start(f32[192,512]{1,0:T(8,128)S(1)} %get-tuple-element.37), channel_id=1, source_target_pairs={{0,1},{1,0},{2,33},{3,32},{4,5},{5,4},{6,37},{7,36},{8,9},{9,8},{1... | collective-permute-start | bytes 1179656 | tf_op jit(solution)/shard_map/ppermute | solution.py:72
  198.6 1.9 collective-permute-start.29
  201.5 4.8 %collective-permute-start.46 = (f32[192,512]{1,0:T(8,128)S(1)}, f32[192,512]{1,0:T(8,128)S(1)}, u32[]{:S(2)}, u32[]{:S(2)}) collective-permute-start(f32[192,512]{1,0:T(8,128)S(1)} %get-tuple-element.24), channel_id=1, source_target_pairs={{0,0},{1,1},{2,32},{3,33},{4,4},{5,5},{6,36},{7,37},{8,8},{9,9},{1... | collective-permute-start | bytes 1179656 | tf_op jit(solution)/shard_map/ppermute | solution.py:72
  206.3 6.9 %collective-permute-done.29 = f32[192,512]{1,0:T(8,128)S(1)} collective-permute-done((f32[192,512]{1,0:T(8,128)S(1)}, f32[192,512]{1,0:T(8,128)S(1)}, u32[]{:S(2)}, u32[]{:S(2)}) %collective-permute-start.29) | collective-permute-done | bytes 393248 | tf_op jit(solution)/shard_map/ppermute | solution.py:72
  213.4 4.4 %collective-permute-done.45 = f32[192,512]{1,0:T(8,128)S(1)} collective-permute-done((f32[192,512]{1,0:T(8,128)S(1)}, f32[192,512]{1,0:T(8,128)S(1)}, u32[]{:S(2)}, u32[]{:S(2)}) %collective-permute-start.45) | collective-permute-done | bytes 393248 | tf_op jit(solution)/shard_map/ppermute | solution.py:72
  217.9 4.9 %collective-permute-done.30 = f32[192,512]{1,0:T(8,128)S(1)} collective-permute-done((f32[192,512]{1,0:T(8,128)S(1)}, f32[192,512]{1,0:T(8,128)S(1)}, u32[]{:S(2)}, u32[]{:S(2)}) %collective-permute-start.30) | collective-permute-done | bytes 393248 | tf_op jit(solution)/shard_map/ppermute | solution.py:72
  223.8 1.0 fusion.80
  224.8 2.3 collective-permute-done.47
  228.0 0.9 fusion.75
  229.0 5.5 %expand.2.rest_0_ = f32[2,1024,1024]{2,1,0:T(8,128)} custom-call(s32[1]{0:T(128)} %constant.63.clone.1.flag, f32[2,192,1024]{2,1,0:T(8,128)} %bitcast.159, f32[192,512]{1,0:T(8,128)} %get-tuple-element.22.r0_ref, f32[192,512]{1,0:T(8,128)} %get-tuple-element.21.r1_ref), custom_call_target="tpu_custom_call" | custom-call | flops 402653184 | bytes 6553600 | tf_op jit(solution)/shard_map/expand/pallas_call | solution.py:120
  234.4 5.5 %expand.3 = f32[2,1024,1024]{2,1,0:T(8,128)} custom-call(s32[1]{0:T(128)} %constant.63.clone.1.flag, f32[2,192,1024]{2,1,0:T(8,128)} %bitcast.160, f32[192,512]{1,0:T(8,128)} %get-tuple-element.36.r0_ref, f32[192,512]{1,0:T(8,128)} %get-tuple-element.35.r1_ref, f32[2,1024,1024]{2,1,0:T(8,128)} %expand.2.rest_0_), custom_call_target="tpu_custom_call", output_to_operand_aliasing={{}: (4, {})} | custom-call | flops 402653184 | bytes 6553600 | tf_op jit(solution)/shard_map/expand/pallas_call | solution.py:120
  (135 shorter events, 24.7 us)
Async XLA Ops:
  0.0 2.8 %copy-start = (f32[2,1,1024,192]{2,3,1,0:T(8,128)S(1)}, f32[2,1,1024,192]{2,3,1,0:T(8,128)}, u32[]{:S(2)}) copy-start(f32[2,1,1024,192]{2,3,1,0:T(8,128)} %param.5) | copy-start | bytes 4718596
  6.2 67.5 %collective-permute-start.4 = (f32[192,512]{1,0:T(8,128)}, f32[192,512]{1,0:T(8,128)S(1)}, u32[]{:S(2)}, u32[]{:S(2)}) collective-permute-start(f32[192,512]{1,0:T(8,128)} %get-tuple-element.59), channel_id=1, source_target_pairs={{0,0},{1,1},{2,32},{3,33},{4,4},{5,5},{6,36},{7,37},{8,8},{9,9},{1... | collective-permute-start | bytes 1179656 | tf_op jit(solution)/shard_map/ppermute | solution.py:72
  17.0 24.4 %collective-permute-start.12 = (f32[1,2,192,192]{3,2,1,0:T(8,128)}, f32[1,2,192,192]{3,2,1,0:T(8,128)}, u32[]{:S(2)}, u32[]{:S(2)}) collective-permute-start(f32[1,2,192,192]{3,2,1,0:T(8,128)} %get-tuple-element.41), channel_id=1, source_target_pairs={{0,64},{1,65},{2,66},{3,67},{4,80},{5,81},{6,82},{7,83},{8,72},{9,... | collective-permute-start | bytes 884744 | tf_op jit(solution)/shard_map/ppermute | solution.py:72
  21.6 20.5 %collective-permute-start.13 = (f32[1,2,192,192]{3,2,1,0:T(8,128)}, f32[1,2,192,192]{3,2,1,0:T(8,128)}, u32[]{:S(2)}, u32[]{:S(2)}) collective-permute-start(f32[1,2,192,192]{3,2,1,0:T(8,128)} %get-tuple-element.42), channel_id=1, source_target_pairs={{0,0},{1,1},{2,2},{3,3},{4,16},{5,17},{6,18},{7,19},{8,8},{9,9},{1... | collective-permute-start | bytes 884744 | tf_op jit(solution)/shard_map/ppermute | solution.py:72
  25.7 21.2 %collective-permute-start.2 = (f32[1,2,192,192]{3,2,1,0:T(8,128)}, f32[1,2,192,192]{3,2,1,0:T(8,128)}, u32[]{:S(2)}, u32[]{:S(2)}) collective-permute-start(f32[1,2,192,192]{3,2,1,0:T(8,128)} %get-tuple-element.63), channel_id=1, source_target_pairs={{0,1},{1,0},{2,33},{3,32},{4,5},{5,4},{6,37},{7,36},{8,9},{9,8},{1... | collective-permute-start | bytes 884744 | tf_op jit(solution)/shard_map/ppermute | solution.py:72
  26.7 21.3 %collective-permute-start.3 = (f32[1,2,192,192]{3,2,1,0:T(8,128)}, f32[1,2,192,192]{3,2,1,0:T(8,128)}, u32[]{:S(2)}, u32[]{:S(2)}) collective-permute-start(f32[1,2,192,192]{3,2,1,0:T(8,128)} %get-tuple-element.64), channel_id=1, source_target_pairs={{0,0},{1,1},{2,32},{3,33},{4,4},{5,5},{6,36},{7,37},{8,8},{9,9},{1... | collective-permute-start | bytes 884744 | tf_op jit(solution)/shard_map/ppermute | solution.py:72
  32.6 1.4 copy-start.1
  34.0 5.6 %slice-start.2 = ((f32[8,2,1,2,192,192]{5,4,3,2,1,0:T(8,128)}), f32[3,2,1,2,192,192]{5,4,3,2,1,0:T(8,128)S(1)}, s32[]{:S(2)}) async-start(f32[8,2,1,2,192,192]{5,4,3,2,1,0:T(8,128)} %param.6), calls=%async_computation.2 | async-start | bytes 4718592 | tf_op jit(solution)/shard_map/slice | solution.py:164
  41.4 13.8 %collective-permute-start = (f32[1,2,192,192]{3,2,1,0:T(8,128)}, f32[1,2,192,192]{3,2,1,0:T(8,128)S(1)}, u32[]{:S(2)}, u32[]{:S(2)}) collective-permute-start(f32[1,2,192,192]{3,2,1,0:T(8,128)} %get-tuple-element.57), channel_id=1, source_target_pairs={{0,1},{1,33},{2,0},{3,32},{4,5},{5,37},{6,4},{7,36},{8,9},{9,41},{... | collective-permute-start | bytes 884744 | tf_op jit(solution)/shard_map/ppermute | solution.py:72
  42.1 14.4 %collective-permute-start.1 = (f32[1,2,192,192]{3,2,1,0:T(8,128)}, f32[1,2,192,192]{3,2,1,0:T(8,128)S(1)}, u32[]{:S(2)}, u32[]{:S(2)}) collective-permute-start(f32[1,2,192,192]{3,2,1,0:T(8,128)} %get-tuple-element.58), channel_id=1, source_target_pairs={{0,0},{1,32},{2,1},{3,33},{4,4},{5,36},{6,5},{7,37},{8,8},{9,40},{... | collective-permute-start | bytes 884744 | tf_op jit(solution)/shard_map/ppermute | solution.py:72
  46.9 16.1 %collective-permute-start.14 = (f32[1,2,192,192]{3,2,1,0:T(8,128)S(1)}, f32[1,2,192,192]{3,2,1,0:T(8,128)S(1)}, u32[]{:S(2)}, u32[]{:S(2)}) collective-permute-start(f32[1,2,192,192]{3,2,1,0:T(8,128)S(1)} %get-tuple-element.47), channel_id=1, source_target_pairs={{0,64},{1,65},{2,66},{3,67},{4,80},{5,81},{6,82},{7,83},{8,72},{9,... | collective-permute-start | bytes 884744 | tf_op jit(solution)/shard_map/ppermute | solution.py:72
  48.0 7.2 %copy-start.4 = (f32[192,512]{1,0:T(8,128)S(1)}, f32[192,512]{1,0:T(8,128)}, u32[]{:S(2)}) copy-start(f32[192,512]{1,0:T(8,128)} %get-tuple-element.60) | copy-start | bytes 1179652
  48.0 8.5 %copy-start.5 = (f32[192,512]{1,0:T(8,128)S(1)}, f32[192,512]{1,0:T(8,128)}, u32[]{:S(2)}) copy-start(f32[192,512]{1,0:T(8,128)} %get-tuple-element.33) | copy-start | bytes 1179652
  48.0 21.8 %collective-permute-start.15 = (f32[1,2,192,192]{3,2,1,0:T(8,128)S(1)}, f32[1,2,192,192]{3,2,1,0:T(8,128)S(1)}, u32[]{:S(2)}, u32[]{:S(2)}) collective-permute-start(f32[1,2,192,192]{3,2,1,0:T(8,128)S(1)} %get-tuple-element.48), channel_id=1, source_target_pairs={{0,0},{1,1},{2,2},{3,3},{4,16},{5,17},{6,18},{7,19},{8,8},{9,9},{1... | collective-permute-start | bytes 884744 | tf_op jit(solution)/shard_map/ppermute | solution.py:72
  55.1 7.8 %copy-start.6 = (f32[192,512]{1,0:T(8,128)S(1)}, f32[192,512]{1,0:T(8,128)}, u32[]{:S(2)}) copy-start(f32[192,512]{1,0:T(8,128)} %get-tuple-element.34) | copy-start | bytes 1179652
  55.1 14.7 %copy-start.3 = (f32[3,2,192,192]{3,2,1,0:T(8,128)S(1)}, f32[3,2,192,192]{3,2,1,0:T(8,128)}, u32[]{:S(2)}) copy-start(f32[3,2,192,192]{3,2,1,0:T(8,128)} %get-tuple-element.17) | copy-start | bytes 2654212
  55.2 14.8 %collective-permute-start.5 = (f32[192,512]{1,0:T(8,128)S(1)}, f32[192,512]{1,0:T(8,128)S(1)}, u32[]{:S(2)}, u32[]{:S(2)}) collective-permute-start(f32[192,512]{1,0:T(8,128)S(1)} %copy-done.4), channel_id=1, source_target_pairs={{0,1},{1,0},{2,33},{3,32},{4,5},{5,4},{6,37},{7,36},{8,9},{9,8},{1... | collective-permute-start | bytes 1179656 | tf_op jit(solution)/shard_map/ppermute | solution.py:72
  56.5 18.3 %collective-permute-start.31 = (f32[192,512]{1,0:T(8,128)S(1)}, f32[192,512]{1,0:T(8,128)S(1)}, u32[]{:S(2)}, u32[]{:S(2)}) collective-permute-start(f32[192,512]{1,0:T(8,128)S(1)} %copy-done.5), channel_id=1, source_target_pairs={{0,0},{1,1},{2,32},{3,33},{4,4},{5,5},{6,36},{7,37},{8,8},{9,9},{1... | collective-permute-start | bytes 1179656 | tf_op jit(solution)/shard_map/ppermute | solution.py:72
  62.9 11.4 %collective-permute-start.32 = (f32[192,512]{1,0:T(8,128)S(1)}, f32[192,512]{1,0:T(8,128)S(1)}, u32[]{:S(2)}, u32[]{:S(2)}) collective-permute-start(f32[192,512]{1,0:T(8,128)S(1)} %copy-done.6), channel_id=1, source_target_pairs={{0,1},{1,0},{2,33},{3,32},{4,5},{5,4},{6,37},{7,36},{8,9},{9,8},{1... | collective-permute-start | bytes 1179656 | tf_op jit(solution)/shard_map/ppermute | solution.py:72
  69.8 1.3 copy-start.2
  69.8 27.8 %collective-permute-start.17 = (f32[3,2,192,192]{3,2,1,0:T(8,128)S(1)}, f32[3,2,192,192]{3,2,1,0:T(8,128)S(1)}, u32[]{:S(2)}, u32[]{:S(2)}) collective-permute-start(f32[3,2,192,192]{3,2,1,0:T(8,128)S(1)} %copy-done.3), channel_id=1, source_target_pairs={{0,64},{1,65},{2,66},{3,67},{4,0},{5,1},{6,2},{7,3},{8,72},{9,73},... | collective-permute-start | bytes 2654216 | tf_op jit(solution)/shard_map/ppermute | solution.py:72
  71.1 28.6 %collective-permute-start.16 = (f32[3,2,192,192]{3,2,1,0:T(8,128)S(1)}, f32[3,2,192,192]{3,2,1,0:T(8,128)S(1)}, u32[]{:S(2)}, u32[]{:S(2)}) collective-permute-start(f32[3,2,192,192]{3,2,1,0:T(8,128)S(1)} %copy-done.2), channel_id=1, source_target_pairs={{0,0},{1,1},{2,2},{3,3},{4,64},{5,65},{6,66},{7,67},{8,8},{9,9},{1... | collective-permute-start | bytes 2654216 | tf_op jit(solution)/shard_map/ppermute | solution.py:72
  75.3 8.7 %collective-permute-start.33 = (f32[192,512]{1,0:T(8,128)S(1)}, f32[192,512]{1,0:T(8,128)S(1)}, u32[]{:S(2)}, u32[]{:S(2)}) collective-permute-start(f32[192,512]{1,0:T(8,128)S(1)} %slice.410), channel_id=1, source_target_pairs={{0,32},{1,33},{2,34},{3,35},{4,36},{5,37},{6,38},{7,39},{8,40},{9,... | collective-permute-start | bytes 1179656 | tf_op jit(solution)/shard_map/ppermute | solution.py:72
  75.4 2.3 collective-permute-start.6
  78.2 22.3 %collective-permute-start.8 = (f32[192,512]{1,0:T(8,128)S(1)}, f32[192,512]{1,0:T(8,128)S(1)}, u32[]{:S(2)}, u32[]{:S(2)}) collective-permute-start(f32[192,512]{1,0:T(8,128)S(1)} %get-tuple-element.53), channel_id=1, source_target_pairs={{0,2},{1,34},{2,0},{3,32},{4,6},{5,38},{6,4},{7,36},{8,10},{9,42},... | collective-permute-start | bytes 1179656 | tf_op jit(solution)/shard_map/ppermute | solution.py:72
  81.9 19.5 %collective-permute-start.7 = (f32[192,512]{1,0:T(8,128)S(1)}, f32[192,512]{1,0:T(8,128)S(1)}, u32[]{:S(2)}, u32[]{:S(2)}) collective-permute-start(f32[192,512]{1,0:T(8,128)S(1)} %get-tuple-element.54), channel_id=1, source_target_pairs={{0,0},{1,32},{2,2},{3,34},{4,4},{5,36},{6,6},{7,38},{8,8},{9,40},{... | collective-permute-start | bytes 1179656 | tf_op jit(solution)/shard_map/ppermute | solution.py:72
  84.0 38.3 %slice-start = ((s8[6291456]{0:T(1024)(128)(4,1)}), s8[2097152]{0:T(1024)(128)(4,1)S(1)}, s32[]{:S(2)}) async-start(s8[6291456]{0:T(1024)(128)(4,1)} %bitcast.157), calls=%async_computation | async-start | bytes 4194304
  84.5 21.7 %collective-permute-start.34 = (f32[192,512]{1,0:T(8,128)S(1)}, f32[192,512]{1,0:T(8,128)S(1)}, u32[]{:S(2)}, u32[]{:S(2)}) collective-permute-start(f32[192,512]{1,0:T(8,128)S(1)} %get-tuple-element.31), channel_id=1, source_target_pairs={{0,2},{1,34},{2,0},{3,32},{4,6},{5,38},{6,4},{7,36},{8,10},{9,42},... | collective-permute-start | bytes 1179656 | tf_op jit(solution)/shard_map/ppermute | solution.py:72
  97.6 10.6 %collective-permute-start.35 = (f32[192,512]{1,0:T(8,128)S(1)}, f32[192,512]{1,0:T(8,128)S(1)}, u32[]{:S(2)}, u32[]{:S(2)}) collective-permute-start(f32[192,512]{1,0:T(8,128)S(1)} %get-tuple-element.32), channel_id=1, source_target_pairs={{0,0},{1,32},{2,2},{3,34},{4,4},{5,36},{6,6},{7,38},{8,8},{9,40},{... | collective-permute-start | bytes 1179656 | tf_op jit(solution)/shard_map/ppermute | solution.py:72
  99.9 22.3 %slice-start.1 = ((s8[6291456]{0:T(1024)(128)(4,1)}), s8[4194304]{0:T(1024)(128)(4,1)S(1)}, s32[]{:S(2)}) async-start(s8[6291456]{0:T(1024)(128)(4,1)} %bitcast.157), calls=%async_computation.1 | async-start | bytes 8388608
  99.9 19.0 %collective-permute-start.18 = (f32[2,2,192,192]{3,2,1,0:T(8,128)S(1)}, f32[2,2,192,192]{3,2,1,0:T(8,128)S(1)}, u32[]{:S(2)}, u32[]{:S(2)}) collective-permute-start(f32[2,2,192,192]{3,2,1,0:T(8,128)S(1)} %get-tuple-element.13), channel_id=1, source_target_pairs={{0,16},{1,17},{2,18},{3,19},{4,20},{5,21},{6,22},{7,23},{8,48},{9,... | collective-permute-start | bytes 1769480 | tf_op jit(solution)/shard_map/ppermute | solution.py:72
  100.5 21.7 %collective-permute-start.19 = (f32[2,2,192,192]{3,2,1,0:T(8,128)S(1)}, f32[2,2,192,192]{3,2,1,0:T(8,128)S(1)}, u32[]{:S(2)}, u32[]{:S(2)}) collective-permute-start(f32[2,2,192,192]{3,2,1,0:T(8,128)S(1)} %get-tuple-element.14), channel_id=1, source_target_pairs={{0,0},{1,1},{2,2},{3,3},{4,4},{5,5},{6,6},{7,7},{8,32},{9,33},{10,... | collective-permute-start | bytes 1769480 | tf_op jit(solution)/shard_map/ppermute | solution.py:72
  101.5 27.8 %collective-permute-start.20 = (f32[192,512]{1,0:T(8,128)S(1)}, f32[192,512]{1,0:T(8,128)S(1)}, u32[]{:S(2)}, u32[]{:S(2)}) collective-permute-start(f32[192,512]{1,0:T(8,128)S(1)} %get-tuple-element.51), channel_id=1, source_target_pairs={{0,0},{1,1},{2,2},{3,3},{4,4},{5,5},{6,6},{7,7},{8,8},{9,9},{10,10... | collective-permute-start | bytes 1179656 | tf_op jit(solution)/shard_map/ppermute | solution.py:72
  106.3 16.0 %collective-permute-start.9 = (f32[192,512]{1,0:T(8,128)S(1)}, f32[192,512]{1,0:T(8,128)S(1)}, u32[]{:S(2)}, u32[]{:S(2)}) collective-permute-start(f32[192,512]{1,0:T(8,128)S(1)} %get-tuple-element.52), channel_id=1, source_target_pairs={{0,4},{1,5},{2,6},{3,7},{4,0},{5,1},{6,2},{7,3},{8,12},{9,13},{10,... | collective-permute-start | bytes 1179656 | tf_op jit(solution)/shard_map/ppermute | solution.py:72
  108.4 24.3 %collective-permute-start.36 = (f32[192,512]{1,0:T(8,128)S(1)}, f32[192,512]{1,0:T(8,128)S(1)}, u32[]{:S(2)}, u32[]{:S(2)}) collective-permute-start(f32[192,512]{1,0:T(8,128)S(1)} %get-tuple-element.29), channel_id=1, source_target_pairs={{0,0},{1,1},{2,2},{3,3},{4,4},{5,5},{6,6},{7,7},{8,8},{9,9},{10,10... | collective-permute-start | bytes 1179656 | tf_op jit(solution)/shard_map/ppermute | solution.py:72
  118.9 13.3 %collective-permute-start.37 = (f32[192,512]{1,0:T(8,128)S(1)}, f32[192,512]{1,0:T(8,128)S(1)}, u32[]{:S(2)}, u32[]{:S(2)}) collective-permute-start(f32[192,512]{1,0:T(8,128)S(1)} %get-tuple-element.30), channel_id=1, source_target_pairs={{0,4},{1,5},{2,6},{3,7},{4,0},{5,1},{6,2},{7,3},{8,12},{9,13},{10,... | collective-permute-start | bytes 1179656 | tf_op jit(solution)/shard_map/ppermute | solution.py:72
  122.3 20.1 %collective-permute-start.10 = (f32[1,2,192,192]{3,2,1,0:T(8,128)S(1)}, f32[1,2,192,192]{3,2,1,0:T(8,128)S(1)}, u32[]{:S(2)}, u32[]{:S(2)}) collective-permute-start(f32[1,2,192,192]{3,2,1,0:T(8,128)S(1)} %get-tuple-element.7), channel_id=1, source_target_pairs={{0,0},{1,64},{2,32},{3,96},{4,16},{5,80},{6,48},{7,112},{8,8},{9,7... | collective-permute-start | bytes 884744 | tf_op jit(solution)/shard_map/ppermute | solution.py:72
  133.2 21.7 %collective-permute-start.40 = (f32[192,512]{1,0:T(8,128)S(1)}, f32[192,512]{1,0:T(8,128)S(1)}, u32[]{:S(2)}, u32[]{:S(2)}) collective-permute-start(f32[192,512]{1,0:T(8,128)S(1)} %get-tuple-element.27), channel_id=1, source_target_pairs={{0,16},{1,17},{2,18},{3,19},{4,20},{5,21},{6,22},{7,23},{8,48},{9,... | collective-permute-start | bytes 1179656 | tf_op jit(solution)/shard_map/ppermute | solution.py:72
  133.3 21.7 %collective-permute-start.38 = (f32[192,512]{1,0:T(8,128)S(1)}, f32[192,512]{1,0:T(8,128)S(1)}, u32[]{:S(2)}, u32[]{:S(2)}) collective-permute-start(f32[192,512]{1,0:T(8,128)S(1)} %get-tuple-element.28), channel_id=1, source_target_pairs={{0,0},{1,1},{2,2},{3,3},{4,4},{5,5},{6,6},{7,7},{8,32},{9,33},{10,... | collective-permute-start | bytes 1179656 | tf_op jit(solution)/shard_map/ppermute | solution.py:72
  134.0 22.4 %collective-permute-start.23 = (f32[192,512]{1,0:T(8,128)S(1)}, f32[192,512]{1,0:T(8,128)S(1)}, u32[]{:S(2)}, u32[]{:S(2)}) collective-permute-start(f32[192,512]{1,0:T(8,128)S(1)} %get-tuple-element.49), channel_id=1, source_target_pairs={{0,16},{1,17},{2,18},{3,19},{4,20},{5,21},{6,22},{7,23},{8,48},{9,... | collective-permute-start | bytes 1179656 | tf_op jit(solution)/shard_map/ppermute | solution.py:72
  137.1 20.3 %collective-permute-start.21 = (f32[192,512]{1,0:T(8,128)S(1)}, f32[192,512]{1,0:T(8,128)S(1)}, u32[]{:S(2)}, u32[]{:S(2)}) collective-permute-start(f32[192,512]{1,0:T(8,128)S(1)} %get-tuple-element.50), channel_id=1, source_target_pairs={{0,0},{1,1},{2,2},{3,3},{4,4},{5,5},{6,6},{7,7},{8,32},{9,33},{10,... | collective-permute-start | bytes 1179656 | tf_op jit(solution)/shard_map/ppermute | solution.py:72
  142.4 70.9 %collective-permute-start.11 = (f32[1,2,192,192]{3,2,1,0:T(8,128)S(1)}, f32[1,2,192,192]{3,2,1,0:T(8,128)S(1)}, u32[]{:S(2)}, u32[]{:S(2)}) collective-permute-start(f32[1,2,192,192]{3,2,1,0:T(8,128)S(1)} %get-tuple-element.8), channel_id=1, source_target_pairs={{0,0},{1,64},{2,32},{3,96},{4,16},{5,80},{6,48},{7,112},{8,8},{9,7... | collective-permute-start | bytes 884744 | tf_op jit(solution)/shard_map/ppermute | solution.py:72
  154.9 9.8 %collective-permute-start.41 = (f32[192,512]{1,0:T(8,128)S(1)}, f32[192,512]{1,0:T(8,128)S(1)}, u32[]{:S(2)}, u32[]{:S(2)}) collective-permute-start(f32[192,512]{1,0:T(8,128)S(1)} %collective-permute-done.40), channel_id=1, source_target_pairs={{0,32},{1,33},{2,34},{3,35},{4,36},{5,37},{6,38},{7,39},{8,40},{9,... | collective-permute-start | bytes 1179656 | tf_op jit(solution)/shard_map/ppermute | solution.py:72
  155.0 8.7 %collective-permute-start.39 = (f32[192,512]{1,0:T(8,128)S(1)}, f32[192,512]{1,0:T(8,128)S(1)}, u32[]{:S(2)}, u32[]{:S(2)}) collective-permute-start(f32[192,512]{1,0:T(8,128)S(1)} %collective-permute-done.38), channel_id=1, source_target_pairs={{0,32},{1,33},{2,34},{3,35},{4,36},{5,37},{6,38},{7,39},{8,40},{9,... | collective-permute-start | bytes 1179656 | tf_op jit(solution)/shard_map/ppermute | solution.py:72
  156.3 4.0 %collective-permute-start.24 = (f32[192,512]{1,0:T(8,128)S(1)}, f32[192,512]{1,0:T(8,128)S(1)}, u32[]{:S(2)}, u32[]{:S(2)}) collective-permute-start(f32[192,512]{1,0:T(8,128)S(1)} %collective-permute-done.23), channel_id=1, source_target_pairs={{0,32},{1,33},{2,34},{3,35},{4,36},{5,37},{6,38},{7,39},{8,40},{9,... | collective-permute-start | bytes 1179656 | tf_op jit(solution)/shard_map/ppermute | solution.py:72
  157.4 1.9 collective-permute-start.22
  161.4 13.7 %collective-permute-start.25 = (f32[192,512]{1,0:T(8,128)S(1)}, f32[192,512]{1,0:T(8,128)S(1)}, u32[]{:S(2)}, u32[]{:S(2)}) collective-permute-start(f32[192,512]{1,0:T(8,128)S(1)} %get-tuple-element.43), channel_id=1, source_target_pairs={{0,0},{1,1},{2,2},{3,3},{4,4},{5,5},{6,6},{7,7},{8,32},{9,33},{10,... | collective-permute-start | bytes 1179656 | tf_op jit(solution)/shard_map/ppermute | solution.py:72
  162.1 12.6 %collective-permute-start.26 = (f32[192,512]{1,0:T(8,128)S(1)}, f32[192,512]{1,0:T(8,128)S(1)}, u32[]{:S(2)}, u32[]{:S(2)}) collective-permute-start(f32[192,512]{1,0:T(8,128)S(1)} %get-tuple-element.44), channel_id=1, source_target_pairs={{0,4},{1,5},{2,6},{3,7},{4,0},{5,1},{6,2},{7,3},{8,36},{9,37},{10,... | collective-permute-start | bytes 1179656 | tf_op jit(solution)/shard_map/ppermute | solution.py:72
  165.8 17.8 %collective-permute-start.42 = (f32[192,512]{1,0:T(8,128)S(1)}, f32[192,512]{1,0:T(8,128)S(1)}, u32[]{:S(2)}, u32[]{:S(2)}) collective-permute-start(f32[192,512]{1,0:T(8,128)S(1)} %get-tuple-element.25), channel_id=1, source_target_pairs={{0,0},{1,1},{2,2},{3,3},{4,4},{5,5},{6,6},{7,7},{8,32},{9,33},{10,... | collective-permute-start | bytes 1179656 | tf_op jit(solution)/shard_map/ppermute | solution.py:72
  166.7 16.4 %collective-permute-start.43 = (f32[192,512]{1,0:T(8,128)S(1)}, f32[192,512]{1,0:T(8,128)S(1)}, u32[]{:S(2)}, u32[]{:S(2)}) collective-permute-start(f32[192,512]{1,0:T(8,128)S(1)} %get-tuple-element.26), channel_id=1, source_target_pairs={{0,4},{1,5},{2,6},{3,7},{4,0},{5,1},{6,2},{7,3},{8,36},{9,37},{10,... | collective-permute-start | bytes 1179656 | tf_op jit(solution)/shard_map/ppermute | solution.py:72
  184.1 16.4 %collective-permute-start.44 = (f32[192,512]{1,0:T(8,128)S(1)}, f32[192,512]{1,0:T(8,128)S(1)}, u32[]{:S(2)}, u32[]{:S(2)}) collective-permute-start(f32[192,512]{1,0:T(8,128)S(1)} %slice.418), channel_id=1, source_target_pairs={{0,32},{1,33},{2,34},{3,35},{4,36},{5,37},{6,38},{7,39},{8,40},{9,... | collective-permute-start | bytes 1179656 | tf_op jit(solution)/shard_map/ppermute | solution.py:72
  189.4 1.9 collective-permute-start.27
  191.8 14.4 %collective-permute-start.28 = (f32[192,512]{1,0:T(8,128)S(1)}, f32[192,512]{1,0:T(8,128)S(1)}, u32[]{:S(2)}, u32[]{:S(2)}) collective-permute-start(f32[192,512]{1,0:T(8,128)S(1)} %get-tuple-element.37), channel_id=1, source_target_pairs={{0,1},{1,0},{2,33},{3,32},{4,5},{5,4},{6,37},{7,36},{8,9},{9,8},{1... | collective-permute-start | bytes 1179656 | tf_op jit(solution)/shard_map/ppermute | solution.py:72
  198.6 14.6 %collective-permute-start.29 = (f32[192,512]{1,0:T(8,128)S(1)}, f32[192,512]{1,0:T(8,128)S(1)}, u32[]{:S(2)}, u32[]{:S(2)}) collective-permute-start(f32[192,512]{1,0:T(8,128)S(1)} %get-tuple-element.38), channel_id=1, source_target_pairs={{0,0},{1,1},{2,32},{3,33},{4,4},{5,5},{6,36},{7,37},{8,8},{9,9},{1... | collective-permute-start | bytes 1179656 | tf_op jit(solution)/shard_map/ppermute | solution.py:72
  201.0 16.8 %collective-permute-start.45 = (f32[192,512]{1,0:T(8,128)S(1)}, f32[192,512]{1,0:T(8,128)S(1)}, u32[]{:S(2)}, u32[]{:S(2)}) collective-permute-start(f32[192,512]{1,0:T(8,128)S(1)} %get-tuple-element.23), channel_id=1, source_target_pairs={{0,1},{1,0},{2,33},{3,32},{4,5},{5,4},{6,37},{7,36},{8,9},{9,8},{1... | collective-permute-start | bytes 1179656 | tf_op jit(solution)/shard_map/ppermute | solution.py:72
  201.5 16.3 %collective-permute-start.46 = (f32[192,512]{1,0:T(8,128)S(1)}, f32[192,512]{1,0:T(8,128)S(1)}, u32[]{:S(2)}, u32[]{:S(2)}) collective-permute-start(f32[192,512]{1,0:T(8,128)S(1)} %get-tuple-element.24), channel_id=1, source_target_pairs={{0,0},{1,1},{2,32},{3,33},{4,4},{5,5},{6,36},{7,37},{8,8},{9,9},{1... | collective-permute-start | bytes 1179656 | tf_op jit(solution)/shard_map/ppermute | solution.py:72
  213.2 9.6 %collective-permute-start.30 = (f32[192,512]{1,0:T(8,128)S(1)}, f32[192,512]{1,0:T(8,128)S(1)}, u32[]{:S(2)}, u32[]{:S(2)}) collective-permute-start(f32[192,512]{1,0:T(8,128)S(1)} %broadcast_select_fusion.5), channel_id=1, source_target_pairs={{0,64},{1,65},{2,66},{3,67},{4,68},{5,69},{6,70},{7,71},{8,72},{9,... | collective-permute-start | bytes 1179656 | tf_op jit(solution)/shard_map/ppermute | solution.py:72
  217.9 9.2 %collective-permute-start.47 = (f32[192,512]{1,0:T(8,128)S(1)}, f32[192,512]{1,0:T(8,128)S(1)}, u32[]{:S(2)}, u32[]{:S(2)}) collective-permute-start(f32[192,512]{1,0:T(8,128)S(1)} %broadcast_select_fusion.4), channel_id=1, source_target_pairs={{0,64},{1,65},{2,66},{3,67},{4,68},{5,69},{6,70},{7,71},{8,72},{9,... | collective-permute-start | bytes 1179656 | tf_op jit(solution)/shard_map/ppermute | solution.py:72
where the time goes:
time: 241 us; the launch traced here: 240 us
  starting transfers between devices  108 us (45%)
  waiting for transfers between devices  71.4 us (30%)
  matrix products  29.7 us (12%)
  local copies, waits for them, and re-layouts  15.1 us (6%)
  Pallas kernels  10.9 us (5%)
  other arithmetic  3.45 us (1%)
    ppermute x48, starting transfers between devices, sent(): return lax.ppermute(values, AXES, pairs)  108 us
    ppermute x48, waiting for transfers between devices, sent(): return lax.ppermute(values, AXES, pairs)  71.4 us
    dot_general x36, matrix products, dot(): return jnp.dot(a, b, precision=HIGH if level in FAST_LEVELS else EXACT)  17.4 us
    dot_general x4, matrix products, shards(): lax.dot_general(projector[c, 0], right_sides[c, 0, :, columns], (((0,), (...  12.3 us
    pallas_call x2, Pallas kernels, expand(): pl.pallas_call(expand_kernel, grid_spec=pltpu.PrefetchScalarGridSpec(num_...  10.9 us
    squeeze x6, local copies, waits for them, and re-layouts, fetch(): lax.dynamic_index_in_dim(chosen, bit ^ t, 1, keepdims=False)  6.85 us
  transfers between devices with their start and end apart: 48, of which 16 were waited for; matrix products, arithmetic and copies ran while one was open for 16% of the time, Pallas kernels for 0%

commit v1 on v0

--- a/solution.py
+++ b/solution.py
@@ -202,8 +202,11 @@
     pair = [sent(v, r) for v, r in zip(pair, routes)]
     for index, level in enumerate((3, 4)):
         factors[level] = ([v[index] for v in pair], place)
-    get((5,), list(at_level[5].held))
-    get((6,), list(at_level[6].held))
+    pair, place = fetch(mixing, own, slice(5, 7), list(at_level[5].held))
+    factors[5] = ([v[0] for v in pair], place)
+    place, order, routes = place.to(list(at_level[6].held))
+    pair = ordered([v[1] for v in pair], parity(own, order))
+    factors[6] = ([sent(v, r) for v, r in zip(pair, routes)], place)
     late_mixing = mixing
 
     chunks, starts, start = [], [], 0

time: 241 us -> 266 us (1.10); the launches traced: 240 us -> 261 us
  waiting for transfers between devices: 71.4 us -> 93.5 us
  local copies, waits for them, and re-layouts: 15.1 us -> 10.1 us
  starting transfers between devices: 108 us -> 111 us
    ppermute x48 -> x47, waiting for transfers between devices: 71.4 us -> 93.5 us  [sent(): return lax.ppermute(values, AXES, pairs)]
    squeeze x6 -> x5, local copies, waits for them, and re-layouts: 6.85 us -> 3.29 us  [fetch(): lax.dynamic_index_in_dim(chosen, bit ^ t, 1, keepdims=False)]
    ppermute x48 -> x47, starting transfers between devices: 108 us -> 111 us  [sent(): return lax.ppermute(values, AXES, pairs)]
  transfers between devices with their start and end apart: 48 -> 47, of which waited for: 16 -> 14; matrix products, arithmetic and copies ran while one was open for 16% -> 13% of each run, Pallas kernels for 0% -> 0%
where the time goes in v1:
time: 266 us; the launch traced here: 261 us
  starting transfers between devices  111 us (42%)
  waiting for transfers between devices  93.5 us (35%)
  matrix products  30.6 us (12%)
  Pallas kernels  10.9 us (4%)
  local copies, waits for them, and re-layouts  10.1 us (4%)
  other arithmetic  3.51 us (1%)
    ppermute x47, starting transfers between devices, sent(): return lax.ppermute(values, AXES, pairs)  111 us
    ppermute x47, waiting for transfers between devices, sent(): return lax.ppermute(values, AXES, pairs)  93.5 us
    dot_general x36, matrix products, dot(): return jnp.dot(a, b, precision=HIGH if level in FAST_LEVELS else EXACT)  18.4 us
    dot_general x4, matrix products, shards(): lax.dot_general(projector[c, 0], right_sides[c, 0, :, columns], (((0,), (...  12.2 us
    pallas_call x2, Pallas kernels, expand(): pl.pallas_call(expand_kernel, grid_spec=pltpu.PrefetchScalarGridSpec(num_...  10.9 us
  transfers between devices with their start and end apart: 47, of which 14 were waited for; matrix products, arithmetic and copies ran while one was open for 13% of the time, Pallas kernels for 0%

profile of v1, /device:TPU:7, one launch (start us, length us, event | category | flops | bytes accessed | tf_op | source)
XLA Modules:
  0.0 260.9 jit_solution(3287884574463758840)
XLA Ops:
  0.0 2.8 %fusion.4 = f32[192,512]{1,0:T(8,128)S(1)} fusion(f32[2,1,1024,1024]{3,2,1,0:T(8,128)} %param.4, f32[2,1,1024,192]{2,3,1,0:T(8,128)} %param.5), kind=kOutput, calls=%fused_computation.4 | convolution fusion | flops 603979776 | bytes 3276800 | tf_op jit(solution)/shard_map/dot_general | solution.py:218
  2.8 3.4 %broadcast_select_fusion.5 = (f32[192,512]{1,0:T(8,128)}, f32[192,512]{1,0:T(8,128)}) fusion(f32[192,512]{1,0:T(8,128)S(1)} %fusion.4, pred[]{:T(512)S(6)} %eq.60, f32[2,1,1024,1024]{3,2,1,0:T(8,128)} %param.4, f32[2,1,1024,192]{2,3,1,0:T(8,128)S(1)} %copy-done), kind=kOutput, calls=%fused_computation.133 | convolution fusion | flops 604176384 | bytes 4063233 | tf_op jit(solution)/shard_map/dot_general | solution.py:218
  6.2 5.4 %collective-permute-start.4 = (f32[192,512]{1,0:T(8,128)}, f32[192,512]{1,0:T(8,128)}, u32[]{:S(2)}, u32[]{:S(2)}) collective-permute-start(f32[192,512]{1,0:T(8,128)} %get-tuple-element.56), channel_id=1, source_target_pairs={{0,0},{1,1},{2,32},{3,33},{4,4},{5,5},{6,36},{7,37},{8,8},{9,9},{1... | collective-permute-start | bytes 1179656 | tf_op jit(solution)/shard_map/ppermute | solution.py:72
  11.6 1.5 fusion.74
  13.1 0.9 dynamic-slice_bitcast_fusion.7
  14.6 4.3 %collective-permute-start.1 = (f32[1,2,192,192]{3,2,1,0:T(8,128)}, f32[1,2,192,192]{3,2,1,0:T(8,128)}, u32[]{:S(2)}, u32[]{:S(2)}) collective-permute-start(f32[1,2,192,192]{3,2,1,0:T(8,128)} %get-tuple-element.55), channel_id=1, source_target_pairs={{0,0},{1,32},{2,1},{3,33},{4,4},{5,36},{6,5},{7,37},{8,8},{9,40},{... | collective-permute-start | bytes 884744 | tf_op jit(solution)/shard_map/ppermute | solution.py:72
  18.9 1.0 dynamic-slice_bitcast_fusion.5
  19.9 2.2 collective-permute-start.2
  22.0 1.9 collective-permute-start.3
  24.0 2.5 fusion
  26.5 1.4 copy-done.1
  27.9 3.6 %broadcast_select_fusion.3 = (f32[192,512]{1,0:T(8,128)}, f32[192,512]{1,0:T(8,128)}) fusion(f32[192,512]{1,0:T(8,128)S(1)} %fusion, pred[]{:T(512)S(6)} %eq.60, f32[2,1,1024,1024]{3,2,1,0:T(8,128)} %param.4, f32[2,1,1024,192]{2,3,1,0:T(8,128)S(1)} %copy-done.1), kind=kOutput, calls=%fused_computation.131 | convolution fusion | flops 604176384 | bytes 4063233 | tf_op jit(solution)/shard_map/dot_general | solution.py:218
  31.5 1.2 dynamic-slice_bitcast_fusion
  33.5 0.8 copy-done.3
  34.3 0.8 collective-permute-start.5
  35.1 4.5 %collective-permute-start.30 = (f32[192,512]{1,0:T(8,128)S(1)}, f32[192,512]{1,0:T(8,128)S(1)}, u32[]{:S(2)}, u32[]{:S(2)}) collective-permute-start(f32[192,512]{1,0:T(8,128)S(1)} %copy-done.4), channel_id=1, source_target_pairs={{0,0},{1,1},{2,32},{3,33},{4,4},{5,5},{6,36},{7,37},{8,8},{9,9},{1... | collective-permute-start | bytes 1179656 | tf_op jit(solution)/shard_map/ppermute | solution.py:72
  39.6 1.2 broadcast_select_fusion.9
  40.8 2.3 collective-permute-start.31
  43.1 1.0 collective-permute-start.13
  44.1 1.2 broadcast_select_fusion.7
  45.4 6.7 %collective-permute-done.31 = f32[192,512]{1,0:T(8,128)S(1)} collective-permute-done((f32[192,512]{1,0:T(8,128)}, f32[192,512]{1,0:T(8,128)S(1)}, u32[]{:S(2)}, u32[]{:S(2)}) %collective-permute-start.31) | collective-permute-done | bytes 393248 | tf_op jit(solution)/shard_map/ppermute | solution.py:72
  52.1 6.1 %collective-permute-start.12 = (f32[2,2,192,192]{3,2,1,0:T(8,128)S(1)}, f32[2,2,192,192]{3,2,1,0:T(8,128)S(1)}, u32[]{:S(2)}, u32[]{:S(2)}) collective-permute-start(f32[2,2,192,192]{3,2,1,0:T(8,128)S(1)} %get-tuple-element.23), channel_id=1, source_target_pairs={{0,0},{1,1},{2,2},{3,3},{4,16},{5,17},{6,18},{7,19},{8,8},{9,9},{1... | collective-permute-start | bytes 1769480 | tf_op jit(solution)/shard_map/ppermute | solution.py:72
  59.4 5.3 %collective-permute-start.15 = (f32[3,2,192,192]{3,2,1,0:T(8,128)S(1)}, f32[3,2,192,192]{3,2,1,0:T(8,128)S(1)}, u32[]{:S(2)}, u32[]{:S(2)}) collective-permute-start(f32[3,2,192,192]{3,2,1,0:T(8,128)S(1)} %get-tuple-element.16), channel_id=1, source_target_pairs={{0,0},{1,1},{2,2},{3,3},{4,64},{5,65},{6,66},{7,67},{8,8},{9,9},{1... | collective-permute-start | bytes 2654216 | tf_op jit(solution)/shard_map/ppermute | solution.py:72
  65.1 1.5 convolution_add_fusion.13
  68.3 16.6 %collective-permute-done.12 = f32[2,2,192,192]{3,2,1,0:T(8,128)S(1)} collective-permute-done((f32[2,2,192,192]{3,2,1,0:T(8,128)S(1)}, f32[2,2,192,192]{3,2,1,0:T(8,128)S(1)}, u32[]{:S(2)}, u32[]{:S(2)}) %collective-permute-start.12) | collective-permute-done | bytes 589856 | tf_op jit(solution)/shard_map/ppermute | solution.py:72
  85.8 1.3 collective-permute-start.33
  87.1 2.1 collective-permute-start.34
  89.8 18.0 %collective-permute-done.16 = f32[3,2,192,192]{3,2,1,0:T(8,128)S(1)} collective-permute-done((f32[3,2,192,192]{3,2,1,0:T(8,128)S(1)}, f32[3,2,192,192]{3,2,1,0:T(8,128)S(1)}, u32[]{:S(2)}, u32[]{:S(2)}) %collective-permute-start.16) | collective-permute-done | bytes 884768 | tf_op jit(solution)/shard_map/ppermute | solution.py:72
  107.8 1.7 collective-permute-start.8
  109.5 1.9 collective-permute-start.7
  111.6 5.9 %collective-permute-start.17 = (f32[2,2,192,192]{3,2,1,0:T(8,128)S(1)}, f32[2,2,192,192]{3,2,1,0:T(8,128)S(1)}, u32[]{:S(2)}, u32[]{:S(2)}) collective-permute-start(f32[2,2,192,192]{3,2,1,0:T(8,128)S(1)} %get-tuple-element.11), channel_id=1, source_target_pairs={{0,16},{1,17},{2,18},{3,19},{4,20},{5,21},{6,22},{7,23},{8,48},{9,... | collective-permute-start | bytes 1769480 | tf_op jit(solution)/shard_map/ppermute | solution.py:72
  117.7 1.0 collective-permute-done.8
  118.7 0.8 collective-permute-start.18
  120.0 2.6 collective-permute-start.35
  122.6 2.3 collective-permute-start.36
  124.9 7.6 %collective-permute-done.17 = f32[2,2,192,192]{3,2,1,0:T(8,128)S(1)} collective-permute-done((f32[2,2,192,192]{3,2,1,0:T(8,128)S(1)}, f32[2,2,192,192]{3,2,1,0:T(8,128)S(1)}, u32[]{:S(2)}, u32[]{:S(2)}) %collective-permute-start.17) | collective-permute-done | bytes 589856 | tf_op jit(solution)/shard_map/ppermute | solution.py:72
  132.5 3.4 %collective-permute-start.19 = (f32[192,512]{1,0:T(8,128)S(1)}, f32[192,512]{1,0:T(8,128)S(1)}, u32[]{:S(2)}, u32[]{:S(2)}) collective-permute-start(f32[192,512]{1,0:T(8,128)S(1)} %get-tuple-element.48), channel_id=1, source_target_pairs={{0,0},{1,1},{2,2},{3,3},{4,4},{5,5},{6,6},{7,7},{8,8},{9,9},{10,10... | collective-permute-start | bytes 1179656 | tf_op jit(solution)/shard_map/ppermute | solution.py:72
  136.0 2.8 %collective-permute-start.10 = (f32[1,2,192,192]{3,2,1,0:T(8,128)S(1)}, f32[1,2,192,192]{3,2,1,0:T(8,128)S(1)}, u32[]{:S(2)}, u32[]{:S(2)}) collective-permute-start(f32[1,2,192,192]{3,2,1,0:T(8,128)S(1)} %get-tuple-element.7), channel_id=1, source_target_pairs={{0,0},{1,64},{2,32},{3,96},{4,16},{5,80},{6,48},{7,112},{8,8},{9,7... | collective-permute-start | bytes 884744 | tf_op jit(solution)/shard_map/ppermute | solution.py:72
  139.3 2.5 collective-permute-done.19
  143.5 17.3 %collective-permute-start.39 = (f32[192,512]{1,0:T(8,128)S(1)}, f32[192,512]{1,0:T(8,128)S(1)}, u32[]{:S(2)}, u32[]{:S(2)}) collective-permute-start(f32[192,512]{1,0:T(8,128)S(1)} %get-tuple-element.32), channel_id=1, source_target_pairs={{0,16},{1,17},{2,18},{3,19},{4,20},{5,21},{6,22},{7,23},{8,48},{9,... | collective-permute-start | bytes 1179656 | tf_op jit(solution)/shard_map/ppermute | solution.py:72
  160.8 0.7 collective-permute-start.37
  161.6 1.9 collective-permute-start.11
  163.6 0.7 collective-permute-start.20
  164.3 5.3 %collective-permute-done.39 = f32[192,512]{1,0:T(8,128)S(1)} collective-permute-done((f32[192,512]{1,0:T(8,128)S(1)}, f32[192,512]{1,0:T(8,128)S(1)}, u32[]{:S(2)}, u32[]{:S(2)}) %collective-permute-start.39) | collective-permute-done | bytes 393248 | tf_op jit(solution)/shard_map/ppermute | solution.py:72
  169.6 4.8 %collective-permute-start.40 = (f32[192,512]{1,0:T(8,128)S(1)}, f32[192,512]{1,0:T(8,128)S(1)}, u32[]{:S(2)}, u32[]{:S(2)}) collective-permute-start(f32[192,512]{1,0:T(8,128)S(1)} %collective-permute-done.39), channel_id=1, source_target_pairs={{0,32},{1,33},{2,34},{3,35},{4,36},{5,37},{6,38},{7,39},{8,40},{9,... | collective-permute-start | bytes 1179656 | tf_op jit(solution)/shard_map/ppermute | solution.py:72
  174.4 3.7 %collective-permute-done.22 = f32[192,512]{1,0:T(8,128)S(1)} collective-permute-done((f32[192,512]{1,0:T(8,128)S(1)}, f32[192,512]{1,0:T(8,128)S(1)}, u32[]{:S(2)}, u32[]{:S(2)}) %collective-permute-start.22) | collective-permute-done | bytes 393248 | tf_op jit(solution)/shard_map/ppermute | solution.py:72
  178.1 1.2 collective-permute-start.23
  180.3 5.9 %collective-permute-start.21 = (f32[192,512]{1,0:T(8,128)S(1)}, f32[192,512]{1,0:T(8,128)S(1)}, u32[]{:S(2)}, u32[]{:S(2)}) collective-permute-start(f32[192,512]{1,0:T(8,128)S(1)} %collective-permute-done.20), channel_id=1, source_target_pairs={{0,32},{1,33},{2,34},{3,35},{4,36},{5,37},{6,38},{7,39},{8,40},{9,... | collective-permute-start | bytes 1179656 | tf_op jit(solution)/shard_map/ppermute | solution.py:72
  189.2 0.7 collective-permute-start.41
  192.3 0.7 collective-permute-start.24
  193.0 3.0 %collective-permute-start.25 = (f32[192,512]{1,0:T(8,128)S(1)}, f32[192,512]{1,0:T(8,128)S(1)}, u32[]{:S(2)}, u32[]{:S(2)}) collective-permute-start(f32[192,512]{1,0:T(8,128)S(1)} %get-tuple-element.45), channel_id=1, source_target_pairs={{0,4},{1,5},{2,6},{3,7},{4,0},{5,1},{6,2},{7,3},{8,36},{9,37},{10,... | collective-permute-start | bytes 1179656 | tf_op jit(solution)/shard_map/ppermute | solution.py:72
  196.0 6.6 %collective-permute-done.42 = f32[192,512]{1,0:T(8,128)S(1)} collective-permute-done((f32[192,512]{1,0:T(8,128)S(1)}, f32[192,512]{1,0:T(8,128)S(1)}, u32[]{:S(2)}, u32[]{:S(2)}) %collective-permute-start.42) | collective-permute-done | bytes 393248 | tf_op jit(solution)/shard_map/ppermute | solution.py:72
  204.1 6.9 %collective-permute-done.25 = f32[192,512]{1,0:T(8,128)S(1)} collective-permute-done((f32[192,512]{1,0:T(8,128)S(1)}, f32[192,512]{1,0:T(8,128)S(1)}, u32[]{:S(2)}, u32[]{:S(2)}) %collective-permute-start.25) | collective-permute-done | bytes 393248 | tf_op jit(solution)/shard_map/ppermute | solution.py:72
  214.1 5.5 %collective-permute-start.44 = (f32[192,512]{1,0:T(8,128)S(1)}, f32[192,512]{1,0:T(8,128)S(1)}, u32[]{:S(2)}, u32[]{:S(2)}) collective-permute-start(f32[192,512]{1,0:T(8,128)S(1)} %get-tuple-element.28), channel_id=1, source_target_pairs={{0,1},{1,0},{2,33},{3,32},{4,5},{5,4},{6,37},{7,36},{8,9},{9,8},{1... | collective-permute-start | bytes 1179656 | tf_op jit(solution)/shard_map/ppermute | solution.py:72
  219.6 1.9 collective-permute-start.45
  222.3 5.0 %collective-permute-start.28 = (f32[192,512]{1,0:T(8,128)S(1)}, f32[192,512]{1,0:T(8,128)S(1)}, u32[]{:S(2)}, u32[]{:S(2)}) collective-permute-start(f32[192,512]{1,0:T(8,128)S(1)} %get-tuple-element.43), channel_id=1, source_target_pairs={{0,0},{1,1},{2,32},{3,33},{4,4},{5,5},{6,36},{7,37},{8,8},{9,9},{1... | collective-permute-start | bytes 1179656 | tf_op jit(solution)/shard_map/ppermute | solution.py:72
  227.3 6.8 %collective-permute-done.45 = f32[192,512]{1,0:T(8,128)S(1)} collective-permute-done((f32[192,512]{1,0:T(8,128)S(1)}, f32[192,512]{1,0:T(8,128)S(1)}, u32[]{:S(2)}, u32[]{:S(2)}) %collective-permute-start.45) | collective-permute-done | bytes 393248 | tf_op jit(solution)/shard_map/ppermute | solution.py:72
  234.4 4.5 %collective-permute-done.27 = f32[192,512]{1,0:T(8,128)S(1)} collective-permute-done((f32[192,512]{1,0:T(8,128)S(1)}, f32[192,512]{1,0:T(8,128)S(1)}, u32[]{:S(2)}, u32[]{:S(2)}) %collective-permute-start.27) | collective-permute-done | bytes 393248 | tf_op jit(solution)/shard_map/ppermute | solution.py:72
  239.0 4.8 %collective-permute-done.46 = f32[192,512]{1,0:T(8,128)S(1)} collective-permute-done((f32[192,512]{1,0:T(8,128)S(1)}, f32[192,512]{1,0:T(8,128)S(1)}, u32[]{:S(2)}, u32[]{:S(2)}) %collective-permute-start.46) | collective-permute-done | bytes 393248 | tf_op jit(solution)/shard_map/ppermute | solution.py:72
  244.8 1.0 fusion.75
  245.8 2.3 collective-permute-done.29
  249.0 0.9 fusion.80
  250.0 5.5 %expand.2.rest_0_ = f32[2,1024,1024]{2,1,0:T(8,128)} custom-call(s32[1]{0:T(128)} %constant.59.clone.1.flag, f32[2,192,1024]{2,1,0:T(8,128)} %bitcast.160, f32[192,512]{1,0:T(8,128)} %get-tuple-element.27.r0_ref, f32[192,512]{1,0:T(8,128)} %get-tuple-element.26.r1_ref), custom_call_target="tpu_custom_call" | custom-call | flops 402653184 | bytes 6553600 | tf_op jit(solution)/shard_map/expand/pallas_call | solution.py:120
  255.4 5.5 %expand.3 = f32[2,1024,1024]{2,1,0:T(8,128)} custom-call(s32[1]{0:T(128)} %constant.59.clone.1.flag, f32[2,192,1024]{2,1,0:T(8,128)} %bitcast.161, f32[192,512]{1,0:T(8,128)} %get-tuple-element.41.r0_ref, f32[192,512]{1,0:T(8,128)} %get-tuple-element.40.r1_ref, f32[2,1024,1024]{2,1,0:T(8,128)} %expand.2.rest_0_), custom_call_target="tpu_custom_call", output_to_operand_aliasing={{}: (4, {})} | custom-call | flops 402653184 | bytes 6553600 | tf_op jit(solution)/shard_map/expand/pallas_call | solution.py:120
  (130 shorter events, 22.7 us)
Async XLA Ops:
  0.0 2.8 %copy-start = (f32[2,1,1024,192]{2,3,1,0:T(8,128)S(1)}, f32[2,1,1024,192]{2,3,1,0:T(8,128)}, u32[]{:S(2)}) copy-start(f32[2,1,1024,192]{2,3,1,0:T(8,128)} %param.5) | copy-start | bytes 4718596
  6.2 58.9 %collective-permute-start.4 = (f32[192,512]{1,0:T(8,128)}, f32[192,512]{1,0:T(8,128)}, u32[]{:S(2)}, u32[]{:S(2)}) collective-permute-start(f32[192,512]{1,0:T(8,128)} %get-tuple-element.56), channel_id=1, source_target_pairs={{0,0},{1,1},{2,32},{3,33},{4,4},{5,5},{6,36},{7,37},{8,8},{9,9},{1... | collective-permute-start | bytes 1179656 | tf_op jit(solution)/shard_map/ppermute | solution.py:72
  14.1 19.4 %collective-permute-start = (f32[1,2,192,192]{3,2,1,0:T(8,128)}, f32[1,2,192,192]{3,2,1,0:T(8,128)}, u32[]{:S(2)}, u32[]{:S(2)}) collective-permute-start(f32[1,2,192,192]{3,2,1,0:T(8,128)} %get-tuple-element.54), channel_id=1, source_target_pairs={{0,1},{1,33},{2,0},{3,32},{4,5},{5,37},{6,4},{7,36},{8,9},{9,41},{... | collective-permute-start | bytes 884744 | tf_op jit(solution)/shard_map/ppermute | solution.py:72
  14.6 20.5 %collective-permute-start.1 = (f32[1,2,192,192]{3,2,1,0:T(8,128)}, f32[1,2,192,192]{3,2,1,0:T(8,128)}, u32[]{:S(2)}, u32[]{:S(2)}) collective-permute-start(f32[1,2,192,192]{3,2,1,0:T(8,128)} %get-tuple-element.55), channel_id=1, source_target_pairs={{0,0},{1,32},{2,1},{3,33},{4,4},{5,36},{6,5},{7,37},{8,8},{9,40},{... | collective-permute-start | bytes 884744 | tf_op jit(solution)/shard_map/ppermute | solution.py:72
  19.9 20.9 %collective-permute-start.2 = (f32[1,2,192,192]{3,2,1,0:T(8,128)}, f32[1,2,192,192]{3,2,1,0:T(8,128)}, u32[]{:S(2)}, u32[]{:S(2)}) collective-permute-start(f32[1,2,192,192]{3,2,1,0:T(8,128)} %get-tuple-element.60), channel_id=1, source_target_pairs={{0,1},{1,0},{2,33},{3,32},{4,5},{5,4},{6,37},{7,36},{8,9},{9,8},{1... | collective-permute-start | bytes 884744 | tf_op jit(solution)/shard_map/ppermute | solution.py:72
  22.0 21.0 %collective-permute-start.3 = (f32[1,2,192,192]{3,2,1,0:T(8,128)}, f32[1,2,192,192]{3,2,1,0:T(8,128)}, u32[]{:S(2)}, u32[]{:S(2)}) collective-permute-start(f32[1,2,192,192]{3,2,1,0:T(8,128)} %get-tuple-element.61), channel_id=1, source_target_pairs={{0,0},{1,1},{2,32},{3,33},{4,4},{5,5},{6,36},{7,37},{8,8},{9,9},{1... | collective-permute-start | bytes 884744 | tf_op jit(solution)/shard_map/ppermute | solution.py:72
  26.5 1.4 copy-start.1
  27.9 3.6 %slice-start.3 = ((f32[8,2,1,2,192,192]{5,4,3,2,1,0:T(8,128)}), f32[3,2,1,2,192,192]{5,4,3,2,1,0:T(8,128)S(1)}, s32[]{:S(2)}) async-start(f32[8,2,1,2,192,192]{5,4,3,2,1,0:T(8,128)} %param.6), calls=%async_computation.3 | async-start | bytes 4718592 | tf_op jit(solution)/shard_map/slice | solution.py:164
  31.5 1.8 slice-start.2
  33.3 1.0 copy-start.3
  33.3 1.8 copy-start.4
  34.3 24.5 %collective-permute-start.5 = (f32[192,512]{1,0:T(8,128)S(1)}, f32[192,512]{1,0:T(8,128)S(1)}, u32[]{:S(2)}, u32[]{:S(2)}) collective-permute-start(f32[192,512]{1,0:T(8,128)S(1)} %copy-done.3), channel_id=1, source_target_pairs={{0,1},{1,0},{2,33},{3,32},{4,5},{5,4},{6,37},{7,36},{8,9},{9,8},{1... | collective-permute-start | bytes 1179656 | tf_op jit(solution)/shard_map/ppermute | solution.py:72
  35.1 24.3 %collective-permute-start.30 = (f32[192,512]{1,0:T(8,128)S(1)}, f32[192,512]{1,0:T(8,128)S(1)}, u32[]{:S(2)}, u32[]{:S(2)}) collective-permute-start(f32[192,512]{1,0:T(8,128)S(1)} %copy-done.4), channel_id=1, source_target_pairs={{0,0},{1,1},{2,32},{3,33},{4,4},{5,5},{6,36},{7,37},{8,8},{9,9},{1... | collective-permute-start | bytes 1179656 | tf_op jit(solution)/shard_map/ppermute | solution.py:72
  40.8 11.3 %collective-permute-start.31 = (f32[192,512]{1,0:T(8,128)}, f32[192,512]{1,0:T(8,128)S(1)}, u32[]{:S(2)}, u32[]{:S(2)}) collective-permute-start(f32[192,512]{1,0:T(8,128)} %get-tuple-element.39), channel_id=1, source_target_pairs={{0,1},{1,0},{2,33},{3,32},{4,5},{5,4},{6,37},{7,36},{8,9},{9,8},{1... | collective-permute-start | bytes 1179656 | tf_op jit(solution)/shard_map/ppermute | solution.py:72
  43.1 24.7 %collective-permute-start.13 = (f32[2,2,192,192]{3,2,1,0:T(8,128)S(1)}, f32[2,2,192,192]{3,2,1,0:T(8,128)S(1)}, u32[]{:S(2)}, u32[]{:S(2)}) collective-permute-start(f32[2,2,192,192]{3,2,1,0:T(8,128)S(1)} %get-tuple-element.22), channel_id=1, source_target_pairs={{0,64},{1,65},{2,66},{3,67},{4,80},{5,81},{6,82},{7,83},{8,72},{9,... | collective-permute-start | bytes 1769480 | tf_op jit(solution)/shard_map/ppermute | solution.py:72
  45.3 13.5 %copy-start.2 = (f32[3,2,192,192]{3,2,1,0:T(8,128)S(1)}, f32[3,2,192,192]{3,2,1,0:T(8,128)}, u32[]{:S(2)}) copy-start(f32[3,2,192,192]{3,2,1,0:T(8,128)} %get-tuple-element.15) | copy-start | bytes 2654212
  52.1 32.8 %collective-permute-start.12 = (f32[2,2,192,192]{3,2,1,0:T(8,128)S(1)}, f32[2,2,192,192]{3,2,1,0:T(8,128)S(1)}, u32[]{:S(2)}, u32[]{:S(2)}) collective-permute-start(f32[2,2,192,192]{3,2,1,0:T(8,128)S(1)} %get-tuple-element.23), channel_id=1, source_target_pairs={{0,0},{1,1},{2,2},{3,3},{4,16},{5,17},{6,18},{7,19},{8,8},{9,9},{1... | collective-permute-start | bytes 1769480 | tf_op jit(solution)/shard_map/ppermute | solution.py:72
  58.8 49.0 %collective-permute-start.16 = (f32[3,2,192,192]{3,2,1,0:T(8,128)S(1)}, f32[3,2,192,192]{3,2,1,0:T(8,128)S(1)}, u32[]{:S(2)}, u32[]{:S(2)}) collective-permute-start(f32[3,2,192,192]{3,2,1,0:T(8,128)S(1)} %copy-done.2), channel_id=1, source_target_pairs={{0,64},{1,65},{2,66},{3,67},{4,0},{5,1},{6,2},{7,3},{8,72},{9,73},... | collective-permute-start | bytes 2654216 | tf_op jit(solution)/shard_map/ppermute | solution.py:72
  59.4 50.2 %collective-permute-start.15 = (f32[3,2,192,192]{3,2,1,0:T(8,128)S(1)}, f32[3,2,192,192]{3,2,1,0:T(8,128)S(1)}, u32[]{:S(2)}, u32[]{:S(2)}) collective-permute-start(f32[3,2,192,192]{3,2,1,0:T(8,128)S(1)} %get-tuple-element.16), channel_id=1, source_target_pairs={{0,0},{1,1},{2,2},{3,3},{4,64},{5,65},{6,66},{7,67},{8,8},{9,9},{1... | collective-permute-start | bytes 2654216 | tf_op jit(solution)/shard_map/ppermute | solution.py:72
  66.7 18.5 %collective-permute-start.32 = (f32[192,512]{1,0:T(8,128)S(1)}, f32[192,512]{1,0:T(8,128)S(1)}, u32[]{:S(2)}, u32[]{:S(2)}) collective-permute-start(f32[192,512]{1,0:T(8,128)S(1)} %slice.422), channel_id=1, source_target_pairs={{0,32},{1,33},{2,34},{3,35},{4,36},{5,37},{6,38},{7,39},{8,40},{9,... | collective-permute-start | bytes 1179656 | tf_op jit(solution)/shard_map/ppermute | solution.py:72
  67.8 19.4 %collective-permute-start.6 = (f32[192,512]{1,0:T(8,128)S(1)}, f32[192,512]{1,0:T(8,128)S(1)}, u32[]{:S(2)}, u32[]{:S(2)}) collective-permute-start(f32[192,512]{1,0:T(8,128)S(1)} %slice.374), channel_id=1, source_target_pairs={{0,32},{1,33},{2,34},{3,35},{4,36},{5,37},{6,38},{7,39},{8,40},{9,... | collective-permute-start | bytes 1179656 | tf_op jit(solution)/shard_map/ppermute | solution.py:72
  85.1 26.6 %collective-permute-start.14 = (f32[2,192,192]{2,1,0:T(8,128)S(1)}, f32[2,192,192]{2,1,0:T(8,128)S(1)}, u32[]{:S(2)}, u32[]{:S(2)}) collective-permute-start(f32[2,192,192]{2,1,0:T(8,128)S(1)} %get-tuple-element.19), channel_id=1, source_target_pairs={{0,32},{1,33},{2,34},{3,35},{4,36},{5,37},{6,38},{7,39},{8,40},{9,... | collective-permute-start | bytes 884744 | tf_op jit(solution)/shard_map/ppermute | solution.py:72
  85.8 34.1 %collective-permute-start.33 = (f32[192,512]{1,0:T(8,128)S(1)}, f32[192,512]{1,0:T(8,128)S(1)}, u32[]{:S(2)}, u32[]{:S(2)}) collective-permute-start(f32[192,512]{1,0:T(8,128)S(1)} %get-tuple-element.36), channel_id=1, source_target_pairs={{0,2},{1,34},{2,0},{3,32},{4,6},{5,38},{6,4},{7,36},{8,10},{9,42},... | collective-permute-start | bytes 1179656 | tf_op jit(solution)/shard_map/ppermute | solution.py:72
  87.1 32.8 %collective-permute-start.34 = (f32[192,512]{1,0:T(8,128)S(1)}, f32[192,512]{1,0:T(8,128)S(1)}, u32[]{:S(2)}, u32[]{:S(2)}) collective-permute-start(f32[192,512]{1,0:T(8,128)S(1)} %get-tuple-element.37), channel_id=1, source_target_pairs={{0,0},{1,32},{2,2},{3,34},{4,4},{5,36},{6,6},{7,38},{8,8},{9,40},{... | collective-permute-start | bytes 1179656 | tf_op jit(solution)/shard_map/ppermute | solution.py:72
  107.8 10.9 %collective-permute-start.8 = (f32[192,512]{1,0:T(8,128)S(1)}, f32[192,512]{1,0:T(8,128)S(1)}, u32[]{:S(2)}, u32[]{:S(2)}) collective-permute-start(f32[192,512]{1,0:T(8,128)S(1)} %get-tuple-element.50), channel_id=1, source_target_pairs={{0,2},{1,34},{2,0},{3,32},{4,6},{5,38},{6,4},{7,36},{8,10},{9,42},... | collective-permute-start | bytes 1179656 | tf_op jit(solution)/shard_map/ppermute | solution.py:72
  109.5 10.2 %collective-permute-start.7 = (f32[192,512]{1,0:T(8,128)S(1)}, f32[192,512]{1,0:T(8,128)S(1)}, u32[]{:S(2)}, u32[]{:S(2)}) collective-permute-start(f32[192,512]{1,0:T(8,128)S(1)} %get-tuple-element.51), channel_id=1, source_target_pairs={{0,0},{1,32},{2,2},{3,34},{4,4},{5,36},{6,6},{7,38},{8,8},{9,40},{... | collective-permute-start | bytes 1179656 | tf_op jit(solution)/shard_map/ppermute | solution.py:72
  111.4 24.5 %slice-start = ((s8[6291456]{0:T(1024)(128)(4,1)}), s8[2097152]{0:T(1024)(128)(4,1)S(1)}, s32[]{:S(2)}) async-start(s8[6291456]{0:T(1024)(128)(4,1)} %bitcast.158), calls=%async_computation | async-start | bytes 4194304
  111.6 20.9 %collective-permute-start.17 = (f32[2,2,192,192]{3,2,1,0:T(8,128)S(1)}, f32[2,2,192,192]{3,2,1,0:T(8,128)S(1)}, u32[]{:S(2)}, u32[]{:S(2)}) collective-permute-start(f32[2,2,192,192]{3,2,1,0:T(8,128)S(1)} %get-tuple-element.11), channel_id=1, source_target_pairs={{0,16},{1,17},{2,18},{3,19},{4,20},{5,21},{6,22},{7,23},{8,48},{9,... | collective-permute-start | bytes 1769480 | tf_op jit(solution)/shard_map/ppermute | solution.py:72
  117.7 18.3 %slice-start.1 = ((s8[6291456]{0:T(1024)(128)(4,1)}), s8[4194304]{0:T(1024)(128)(4,1)S(1)}, s32[]{:S(2)}) async-start(s8[6291456]{0:T(1024)(128)(4,1)} %bitcast.158), calls=%async_computation.1 | async-start | bytes 8388608
  118.7 17.1 %collective-permute-start.18 = (f32[2,2,192,192]{3,2,1,0:T(8,128)S(1)}, f32[2,2,192,192]{3,2,1,0:T(8,128)S(1)}, u32[]{:S(2)}, u32[]{:S(2)}) collective-permute-start(f32[2,2,192,192]{3,2,1,0:T(8,128)S(1)} %get-tuple-element.12), channel_id=1, source_target_pairs={{0,0},{1,1},{2,2},{3,3},{4,4},{5,5},{6,6},{7,7},{8,32},{9,33},{10,... | collective-permute-start | bytes 1769480 | tf_op jit(solution)/shard_map/ppermute | solution.py:72
  119.8 16.2 %collective-permute-start.9 = (f32[192,512]{1,0:T(8,128)S(1)}, f32[192,512]{1,0:T(8,128)S(1)}, u32[]{:S(2)}, u32[]{:S(2)}) collective-permute-start(f32[192,512]{1,0:T(8,128)S(1)} %get-tuple-element.49), channel_id=1, source_target_pairs={{0,4},{1,5},{2,6},{3,7},{4,0},{5,1},{6,2},{7,3},{8,12},{9,13},{10,... | collective-permute-start | bytes 1179656 | tf_op jit(solution)/shard_map/ppermute | solution.py:72
  120.0 22.9 %collective-permute-start.35 = (f32[192,512]{1,0:T(8,128)S(1)}, f32[192,512]{1,0:T(8,128)S(1)}, u32[]{:S(2)}, u32[]{:S(2)}) collective-permute-start(f32[192,512]{1,0:T(8,128)S(1)} %get-tuple-element.34), channel_id=1, source_target_pairs={{0,0},{1,1},{2,2},{3,3},{4,4},{5,5},{6,6},{7,7},{8,8},{9,9},{10,10... | collective-permute-start | bytes 1179656 | tf_op jit(solution)/shard_map/ppermute | solution.py:72
  122.6 19.8 %collective-permute-start.36 = (f32[192,512]{1,0:T(8,128)S(1)}, f32[192,512]{1,0:T(8,128)S(1)}, u32[]{:S(2)}, u32[]{:S(2)}) collective-permute-start(f32[192,512]{1,0:T(8,128)S(1)} %get-tuple-element.35), channel_id=1, source_target_pairs={{0,4},{1,5},{2,6},{3,7},{4,0},{5,1},{6,2},{7,3},{8,12},{9,13},{10,... | collective-permute-start | bytes 1179656 | tf_op jit(solution)/shard_map/ppermute | solution.py:72
  132.5 9.4 %collective-permute-start.19 = (f32[192,512]{1,0:T(8,128)S(1)}, f32[192,512]{1,0:T(8,128)S(1)}, u32[]{:S(2)}, u32[]{:S(2)}) collective-permute-start(f32[192,512]{1,0:T(8,128)S(1)} %get-tuple-element.48), channel_id=1, source_target_pairs={{0,0},{1,1},{2,2},{3,3},{4,4},{5,5},{6,6},{7,7},{8,8},{9,9},{10,10... | collective-permute-start | bytes 1179656 | tf_op jit(solution)/shard_map/ppermute | solution.py:72
  136.0 27.5 %collective-permute-start.10 = (f32[1,2,192,192]{3,2,1,0:T(8,128)S(1)}, f32[1,2,192,192]{3,2,1,0:T(8,128)S(1)}, u32[]{:S(2)}, u32[]{:S(2)}) collective-permute-start(f32[1,2,192,192]{3,2,1,0:T(8,128)S(1)} %get-tuple-element.7), channel_id=1, source_target_pairs={{0,0},{1,64},{2,32},{3,96},{4,16},{5,80},{6,48},{7,112},{8,8},{9,7... | collective-permute-start | bytes 884744 | tf_op jit(solution)/shard_map/ppermute | solution.py:72
  143.5 26.2 %collective-permute-start.39 = (f32[192,512]{1,0:T(8,128)S(1)}, f32[192,512]{1,0:T(8,128)S(1)}, u32[]{:S(2)}, u32[]{:S(2)}) collective-permute-start(f32[192,512]{1,0:T(8,128)S(1)} %get-tuple-element.32), channel_id=1, source_target_pairs={{0,16},{1,17},{2,18},{3,19},{4,20},{5,21},{6,22},{7,23},{8,48},{9,... | collective-permute-start | bytes 1179656 | tf_op jit(solution)/shard_map/ppermute | solution.py:72
  160.8 13.6 %collective-permute-start.37 = (f32[192,512]{1,0:T(8,128)S(1)}, f32[192,512]{1,0:T(8,128)S(1)}, u32[]{:S(2)}, u32[]{:S(2)}) collective-permute-start(f32[192,512]{1,0:T(8,128)S(1)} %get-tuple-element.33), channel_id=1, source_target_pairs={{0,0},{1,1},{2,2},{3,3},{4,4},{5,5},{6,6},{7,7},{8,32},{9,33},{10,... | collective-permute-start | bytes 1179656 | tf_op jit(solution)/shard_map/ppermute | solution.py:72
  161.5 16.6 %collective-permute-start.22 = (f32[192,512]{1,0:T(8,128)S(1)}, f32[192,512]{1,0:T(8,128)S(1)}, u32[]{:S(2)}, u32[]{:S(2)}) collective-permute-start(f32[192,512]{1,0:T(8,128)S(1)} %get-tuple-element.46), channel_id=1, source_target_pairs={{0,16},{1,17},{2,18},{3,19},{4,20},{5,21},{6,22},{7,23},{8,48},{9,... | collective-permute-start | bytes 1179656 | tf_op jit(solution)/shard_map/ppermute | solution.py:72
  161.6 72.7 %collective-permute-start.11 = (f32[1,2,192,192]{3,2,1,0:T(8,128)S(1)}, f32[1,2,192,192]{3,2,1,0:T(8,128)S(1)}, u32[]{:S(2)}, u32[]{:S(2)}) collective-permute-start(f32[1,2,192,192]{3,2,1,0:T(8,128)S(1)} %get-tuple-element.8), channel_id=1, source_target_pairs={{0,0},{1,64},{2,32},{3,96},{4,16},{5,80},{6,48},{7,112},{8,8},{9,7... | collective-permute-start | bytes 884744 | tf_op jit(solution)/shard_map/ppermute | solution.py:72
  163.6 16.7 %collective-permute-start.20 = (f32[192,512]{1,0:T(8,128)S(1)}, f32[192,512]{1,0:T(8,128)S(1)}, u32[]{:S(2)}, u32[]{:S(2)}) collective-permute-start(f32[192,512]{1,0:T(8,128)S(1)} %get-tuple-element.47), channel_id=1, source_target_pairs={{0,0},{1,1},{2,2},{3,3},{4,4},{5,5},{6,6},{7,7},{8,32},{9,33},{10,... | collective-permute-start | bytes 1179656 | tf_op jit(solution)/shard_map/ppermute | solution.py:72
  169.6 18.5 %collective-permute-start.40 = (f32[192,512]{1,0:T(8,128)S(1)}, f32[192,512]{1,0:T(8,128)S(1)}, u32[]{:S(2)}, u32[]{:S(2)}) collective-permute-start(f32[192,512]{1,0:T(8,128)S(1)} %collective-permute-done.39), channel_id=1, source_target_pairs={{0,32},{1,33},{2,34},{3,35},{4,36},{5,37},{6,38},{7,39},{8,40},{9,... | collective-permute-start | bytes 1179656 | tf_op jit(solution)/shard_map/ppermute | solution.py:72
  174.4 12.7 %collective-permute-start.38 = (f32[192,512]{1,0:T(8,128)S(1)}, f32[192,512]{1,0:T(8,128)S(1)}, u32[]{:S(2)}, u32[]{:S(2)}) collective-permute-start(f32[192,512]{1,0:T(8,128)S(1)} %collective-permute-done.37), channel_id=1, source_target_pairs={{0,32},{1,33},{2,34},{3,35},{4,36},{5,37},{6,38},{7,39},{8,40},{9,... | collective-permute-start | bytes 1179656 | tf_op jit(solution)/shard_map/ppermute | solution.py:72
  178.1 13.1 %collective-permute-start.23 = (f32[192,512]{1,0:T(8,128)S(1)}, f32[192,512]{1,0:T(8,128)S(1)}, u32[]{:S(2)}, u32[]{:S(2)}) collective-permute-start(f32[192,512]{1,0:T(8,128)S(1)} %collective-permute-done.22), channel_id=1, source_target_pairs={{0,32},{1,33},{2,34},{3,35},{4,36},{5,37},{6,38},{7,39},{8,40},{9,... | collective-permute-start | bytes 1179656 | tf_op jit(solution)/shard_map/ppermute | solution.py:72
  180.3 9.9 %collective-permute-start.21 = (f32[192,512]{1,0:T(8,128)S(1)}, f32[192,512]{1,0:T(8,128)S(1)}, u32[]{:S(2)}, u32[]{:S(2)}) collective-permute-start(f32[192,512]{1,0:T(8,128)S(1)} %collective-permute-done.20), channel_id=1, source_target_pairs={{0,32},{1,33},{2,34},{3,35},{4,36},{5,37},{6,38},{7,39},{8,40},{9,... | collective-permute-start | bytes 1179656 | tf_op jit(solution)/shard_map/ppermute | solution.py:72
  189.2 13.9 %collective-permute-start.41 = (f32[192,512]{1,0:T(8,128)S(1)}, f32[192,512]{1,0:T(8,128)S(1)}, u32[]{:S(2)}, u32[]{:S(2)}) collective-permute-start(f32[192,512]{1,0:T(8,128)S(1)} %get-tuple-element.30), channel_id=1, source_target_pairs={{0,0},{1,1},{2,2},{3,3},{4,4},{5,5},{6,6},{7,7},{8,32},{9,33},{10,... | collective-permute-start | bytes 1179656 | tf_op jit(solution)/shard_map/ppermute | solution.py:72
  189.9 12.7 %collective-permute-start.42 = (f32[192,512]{1,0:T(8,128)S(1)}, f32[192,512]{1,0:T(8,128)S(1)}, u32[]{:S(2)}, u32[]{:S(2)}) collective-permute-start(f32[192,512]{1,0:T(8,128)S(1)} %get-tuple-element.31), channel_id=1, source_target_pairs={{0,4},{1,5},{2,6},{3,7},{4,0},{5,1},{6,2},{7,3},{8,36},{9,37},{10,... | collective-permute-start | bytes 1179656 | tf_op jit(solution)/shard_map/ppermute | solution.py:72
  192.3 19.3 %collective-permute-start.24 = (f32[192,512]{1,0:T(8,128)S(1)}, f32[192,512]{1,0:T(8,128)S(1)}, u32[]{:S(2)}, u32[]{:S(2)}) collective-permute-start(f32[192,512]{1,0:T(8,128)S(1)} %get-tuple-element.44), channel_id=1, source_target_pairs={{0,0},{1,1},{2,2},{3,3},{4,4},{5,5},{6,6},{7,7},{8,32},{9,33},{10,... | collective-permute-start | bytes 1179656 | tf_op jit(solution)/shard_map/ppermute | solution.py:72
  193.0 18.1 %collective-permute-start.25 = (f32[192,512]{1,0:T(8,128)S(1)}, f32[192,512]{1,0:T(8,128)S(1)}, u32[]{:S(2)}, u32[]{:S(2)}) collective-permute-start(f32[192,512]{1,0:T(8,128)S(1)} %get-tuple-element.45), channel_id=1, source_target_pairs={{0,4},{1,5},{2,6},{3,7},{4,0},{5,1},{6,2},{7,3},{8,36},{9,37},{10,... | collective-permute-start | bytes 1179656 | tf_op jit(solution)/shard_map/ppermute | solution.py:72
  203.6 10.0 %collective-permute-start.43 = (f32[192,512]{1,0:T(8,128)S(1)}, f32[192,512]{1,0:T(8,128)S(1)}, u32[]{:S(2)}, u32[]{:S(2)}) collective-permute-start(f32[192,512]{1,0:T(8,128)S(1)} %slice.430), channel_id=1, source_target_pairs={{0,32},{1,33},{2,34},{3,35},{4,36},{5,37},{6,38},{7,39},{8,40},{9,... | collective-permute-start | bytes 1179656 | tf_op jit(solution)/shard_map/ppermute | solution.py:72
  212.1 9.4 %collective-permute-start.26 = (f32[192,512]{1,0:T(8,128)S(1)}, f32[192,512]{1,0:T(8,128)S(1)}, u32[]{:S(2)}, u32[]{:S(2)}) collective-permute-start(f32[192,512]{1,0:T(8,128)S(1)} %slice.416), channel_id=1, source_target_pairs={{0,32},{1,33},{2,34},{3,35},{4,36},{5,37},{6,38},{7,39},{8,40},{9,... | collective-permute-start | bytes 1179656 | tf_op jit(solution)/shard_map/ppermute | solution.py:72
  214.1 13.2 %collective-permute-start.44 = (f32[192,512]{1,0:T(8,128)S(1)}, f32[192,512]{1,0:T(8,128)S(1)}, u32[]{:S(2)}, u32[]{:S(2)}) collective-permute-start(f32[192,512]{1,0:T(8,128)S(1)} %get-tuple-element.28), channel_id=1, source_target_pairs={{0,1},{1,0},{2,33},{3,32},{4,5},{5,4},{6,37},{7,36},{8,9},{9,8},{1... | collective-permute-start | bytes 1179656 | tf_op jit(solution)/shard_map/ppermute | solution.py:72
  219.6 14.5 %collective-permute-start.45 = (f32[192,512]{1,0:T(8,128)S(1)}, f32[192,512]{1,0:T(8,128)S(1)}, u32[]{:S(2)}, u32[]{:S(2)}) collective-permute-start(f32[192,512]{1,0:T(8,128)S(1)} %get-tuple-element.29), channel_id=1, source_target_pairs={{0,0},{1,1},{2,32},{3,33},{4,4},{5,5},{6,36},{7,37},{8,8},{9,9},{1... | collective-permute-start | bytes 1179656 | tf_op jit(solution)/shard_map/ppermute | solution.py:72
  222.1 16.8 %collective-permute-start.27 = (f32[192,512]{1,0:T(8,128)S(1)}, f32[192,512]{1,0:T(8,128)S(1)}, u32[]{:S(2)}, u32[]{:S(2)}) collective-permute-start(f32[192,512]{1,0:T(8,128)S(1)} %get-tuple-element.42), channel_id=1, source_target_pairs={{0,1},{1,0},{2,33},{3,32},{4,5},{5,4},{6,37},{7,36},{8,9},{9,8},{1... | collective-permute-start | bytes 1179656 | tf_op jit(solution)/shard_map/ppermute | solution.py:72
  222.3 16.6 %collective-permute-start.28 = (f32[192,512]{1,0:T(8,128)S(1)}, f32[192,512]{1,0:T(8,128)S(1)}, u32[]{:S(2)}, u32[]{:S(2)}) collective-permute-start(f32[192,512]{1,0:T(8,128)S(1)} %get-tuple-element.43), channel_id=1, source_target_pairs={{0,0},{1,1},{2,32},{3,33},{4,4},{5,5},{6,36},{7,37},{8,8},{9,9},{1... | collective-permute-start | bytes 1179656 | tf_op jit(solution)/shard_map/ppermute | solution.py:72
  234.2 9.6 %collective-permute-start.46 = (f32[192,512]{1,0:T(8,128)S(1)}, f32[192,512]{1,0:T(8,128)S(1)}, u32[]{:S(2)}, u32[]{:S(2)}) collective-permute-start(f32[192,512]{1,0:T(8,128)S(1)} %broadcast_select_fusion), channel_id=1, source_target_pairs={{0,64},{1,65},{2,66},{3,67},{4,68},{5,69},{6,70},{7,71},{8,72},{9,... | collective-permute-start | bytes 1179656 | tf_op jit(solution)/shard_map/ppermute | solution.py:72
  238.9 9.1 %collective-permute-start.29 = (f32[192,512]{1,0:T(8,128)S(1)}, f32[192,512]{1,0:T(8,128)S(1)}, u32[]{:S(2)}, u32[]{:S(2)}) collective-permute-start(f32[192,512]{1,0:T(8,128)S(1)} %broadcast_select_fusion.1), channel_id=1, source_target_pairs={{0,64},{1,65},{2,66},{3,67},{4,68},{5,69},{6,70},{7,71},{8,72},{9,... | collective-permute-start | bytes 1179656 | tf_op jit(solution)/shard_map/ppermute | solution.py:72
